TPU v7x, 128 devices: a whole 4x4x4 slice. The times are simulated.
128 devices in a mesh: gx: 8 (over y, core), gy: 16 (over z, x).
Axes of the slice: x: 4, y: 4, z: 4, core: 2. Of those that a mesh axis runs over, the one named last changes fastest.
Arguments:
- density: bfloat16 [8, 16, 256, 256], P('gx', 'gy'), may hold values from -0.359375 to 0.359375
- neighbours: int32 [8, 16, 256, 24], P('gx', 'gy'), may hold values from 0 to 2303
- correlations: bfloat16 [8, 16, 256, 34560], P('gx', 'gy'), may hold values from -1.5 to 1.5
- weight_first: bfloat16 [8100, 256], replicated, may hold values from -0.0625 to 0.0625
- bias_first: float32 [256], replicated, may hold values from -3 to 3
- weight_second: bfloat16 [256, 256], replicated, may hold values from -0.375 to 0.375
- bias_second: float32 [256], replicated, may hold values from -3 to 3
- weight_third: bfloat16 [256, 256], replicated, may hold values from -0.375 to 0.375
- bias_third: float32 [256], replicated, may hold values from -3 to 3
- readout: float32 [256], replicated, may hold values from -1.5 to 1.5
- destination: int32 [8, 16, 256, 1], P('gx', 'gy'), may hold values from 0 to 127; in each aligned block of 256 rows (0 to 255, 256 to 511, ..., all dimensions but the last counted through in order) at most 4 rows name the same one
Outputs:
- energy: float32 [8, 16, 256], P('gx', 'gy')
- blocks: float32 [128, 128, 4, 256], P(('gx', 'gy'))
Inputs may be any that keep to these rules, and one draw needn't show every extreme that they name: `neighbours`: index n names atom n % 256 of the domain at offset (n // 256 // 3 - 1, n // 256 % 3 - 1) along gx and gy, wrapping around. Devices are numbered gx-major. At most 4 atoms of one domain share a destination, and in every draw some domain has exactly 4 atoms with one destination.
All inputs are finite; a program needn't handle non-finite values.
Results may differ from a plain program's by a relative error of at most 0.0085.
Values may be sent and summed in bfloat16 or wider, within the bound.
A program may use at most 256 MiB of HBM per device.

v0:
```python
import math

import jax
import jax.numpy as jnp
from jax import lax
from jax.sharding import PartitionSpec as P

NPROJ = 90
NORB = 16


def padded(block, sides, width):
    for axis, dim in sides:
        count = lax.axis_size(axis)
        forward = [(i, i + 1) for i in range(count - 1)]
        forward.append((count - 1, 0))
        backward = [(target, source) for source, target in forward]
        low = lax.ppermute(
            lax.slice_in_dim(block, block.shape[dim] - width, None, axis=dim), axis, forward
        )
        high = lax.ppermute(lax.slice_in_dim(block, 0, width, axis=dim), axis, backward)
        block = jnp.concatenate([low, block, high], axis=dim)
    return block


def from_behind(value, axis, steps):
    count = lax.axis_size(axis)
    pairs = [(source, (source + steps) % count) for source in range(count)]
    return lax.ppermute(value, axis, pairs)


def on_device(
    density,
    neighbours,
    correlations,
    weight_first,
    bias_first,
    weight_second,
    bias_second,
    weight_third,
    bias_third,
    readout,
    destination,
):
    atom_count = density.shape[2]
    block_size = density.shape[3]
    neighbour_count = neighbours.shape[3]
    orbitals = NORB
    projectors = NPROJ
    group = math.gcd(atom_count, 32)
    group_count = atom_count // group
    extended = padded(density, (("gx", 0), ("gy", 1)), 1)
    extended = extended.reshape(9 * atom_count, block_size)
    nbr_local = neighbours.reshape(atom_count, neighbour_count)
    gathered = extended[nbr_local].reshape(group_count, group, neighbour_count, orbitals, orbitals)
    projector_all = correlations.reshape(group_count, group, projectors, neighbour_count, orbitals)

    def group_work(inputs):
        grid, projector = inputs
        partial_value = jnp.einsum(
            "apko,akoq->apkq", projector, grid, preferred_element_type=jnp.float32
        ).astype(jnp.bfloat16)
        descriptor = jnp.einsum(
            "apkq,arkq->apr", partial_value, projector, preferred_element_type=jnp.float32
        ).astype(jnp.bfloat16)
        descriptor = descriptor.reshape(group, projectors * projectors)
        pre_first = (
            jnp.dot(descriptor, weight_first, preferred_element_type=jnp.float32) + bias_first
        )
        act_first = jnp.tanh(pre_first)
        pre_second = (
            jnp.dot(
                act_first.astype(jnp.bfloat16), weight_second, preferred_element_type=jnp.float32
            )
            + bias_second
        )
        act_second = act_first + jnp.tanh(pre_second)
        pre_third = (
            jnp.dot(
                act_second.astype(jnp.bfloat16), weight_third, preferred_element_type=jnp.float32
            )
            + bias_third
        )
        act_third = act_second + jnp.tanh(pre_third)
        energy_part = jnp.sum(act_third * readout, axis=-1)
        grad_third = (readout * (1.0 - jnp.tanh(pre_third) ** 2)).astype(jnp.bfloat16)
        back_second = readout + jnp.dot(
            grad_third, weight_third.T, preferred_element_type=jnp.float32
        )
        grad_second = (back_second * (1.0 - jnp.tanh(pre_second) ** 2)).astype(jnp.bfloat16)
        back_first = back_second + jnp.dot(
            grad_second, weight_second.T, preferred_element_type=jnp.float32
        )
        grad_first = (back_first * (1.0 - act_first**2)).astype(jnp.bfloat16)
        slope = jnp.dot(grad_first, weight_first.T, preferred_element_type=jnp.float32).astype(
            jnp.bfloat16
        )
        slope = slope.reshape(group, projectors, projectors)
        lifted = jnp.einsum(
            "apr,arkq->apkq", slope, projector, preferred_element_type=jnp.float32
        ).astype(jnp.bfloat16)
        pair_part = jnp.einsum(
            "apko,apkq->akoq", projector, lifted, preferred_element_type=jnp.float32
        )
        return (energy_part, pair_part.reshape(group, neighbour_count, block_size))

    energy, pair_blocks = lax.map(group_work, (gathered, projector_all))
    energy = energy.reshape(atom_count)
    contrib = jax.ops.segment_sum(
        pair_blocks.reshape(atom_count * neighbour_count, block_size),
        nbr_local.reshape(-1),
        num_segments=9 * atom_count,
    )
    contrib = contrib.reshape(3, 3, atom_count, block_size)
    folded = contrib[1]
    for step_sign in (1, -1):
        folded = folded + from_behind(contrib[1 + step_sign], "gx", step_sign)
    hamilton = folded[1]
    for step_sign in (1, -1):
        hamilton = hamilton + from_behind(folded[1 + step_sign], "gy", step_sign)
    size_x = lax.axis_size("gx")
    size_y = lax.axis_size("gy")
    device_count = size_x * size_y
    slot_count = max(2, 3 * atom_count // (2 * device_count) + 1)
    target = destination.reshape(atom_count)
    order = jnp.arange(atom_count, dtype=jnp.int32)
    same = target[:, None] == target[None, :]
    earlier = order[None, :] < order[:, None]
    slot = jnp.sum(jnp.logical_and(same, earlier).astype(jnp.int32), axis=1)
    position = target * slot_count + slot
    outgoing = (
        jnp.zeros((device_count * slot_count, block_size), jnp.float32).at[position].set(hamilton)
    )
    received = lax.all_to_all(
        outgoing.reshape(device_count, slot_count, block_size),
        ("gx", "gy"),
        split_axis=0,
        concat_axis=0,
        tiled=True,
    )
    return (energy.reshape(1, 1, atom_count), received[None])


def solution(mesh):
    return jax.shard_map(
        on_device,
        mesh=mesh,
        in_specs=(
            P("gx", "gy", None, None),
            P("gx", "gy", None, None),
            P("gx", "gy", None, None),
            P(),
            P(),
            P(),
            P(),
            P(),
            P(),
            P(),
            P("gx", "gy", None, None),
        ),
        out_specs=(P("gx", "gy", None), P(("gx", "gy"), None, None, None)),
        check_vma=False,
    )
```

profile of v0, /device:TPU:1, one launch (start us, length us, event | category | flops | bytes accessed | tf_op | source)
XLA Modules:
  0.0 726.1 jit_solution(4855491250133758493)
XLA Ops:
  9.2 4.8 collective-permute-start.3
  15.0 23.8 %copy.36 = bf16[1,1,256,34560]{2,3,1,0:T(8,128)(2,1)} copy(bf16[1,1,256,34560]{3,2,1,0:T(8,128)(2,1)} %param.15) | data formatting | bytes 35389440 | tf_op args[2]
  38.8 74.6 %reshape.103 = bf16[8,32,90,24,16]{1,0,4,3,2:T(8,128)(2,1)} reshape(bf16[1,1,256,34560]{2,3,1,0:T(8,128)(2,1)} %copy.36) | data formatting | bytes 35389440 | tf_op jit(solution)/shard_map/reshape | solution.py:56
  113.4 80.2 %copy.38 = bf16[8,32,90,24,16]{2,4,3,1,0:T(8,128)(2,1)} copy(bf16[8,32,90,24,16]{1,0,4,3,2:T(8,128)(2,1)} %reshape.103) | data formatting | bytes 35389440 | tf_op jit(solution)/shard_map/while | solution.py:107
  193.9 25.1 %gather_fusion = bf16[6144,256]{1,0:T(8,128)(2,1)} fusion(bf16[2304,256]{1,0:T(8,128)(2,1)S(1)} %bitcast.122, s32[6144]{0:T(1024)S(1)} %broadcast_clamp_fusion), kind=kCustom, calls=%fused_computation | custom fusion | bytes 6316032 | tf_op jit(solution)/shard_map/gather | solution.py:55
  222.2 28.3 %reshape.102 = bf16[8,32,24,16,16]{2,1,0,4,3:T(8,128)(2,1)} reshape(bf16[6144,256]{0,1:T(8,128)(2,1)S(1)} %copy.35) | data formatting | bytes 6291456 | tf_op jit(solution)/shard_map/reshape | solution.py:55
  250.5 390.7 %while.12 = (s32[]{:T(128)}, f32[8,32]{1,0:T(8,128)S(1)}, f32[8,32,24,256]{3,2,1,0:T(8,128)}, bf16[8,32,24,16,16]{2,1,0,4,3:T(8,128)(2,1)}, bf16[8,32,90,24,16]{...) while((s32[]{:T(128)}, f32[8,32]{1,0:T(8,128)S(1)}, ...), condition=%wide.region_2.3_spmd, body=%wide.region_0.2_spmd.sunk | while | flops 754034944 | bytes 40710160 | solution.py:107
  256.6 6.4 copy.48
  263.0 5.3 bitcast_convert_fusion.2
  279.4 4.6 reshape.143
  290.5 5.0 copy.49
  305.4 6.4 copy.48
  311.8 5.3 bitcast_convert_fusion.2
  328.2 4.6 reshape.143
  339.3 5.0 copy.49
  354.3 6.4 copy.48
  360.6 5.3 bitcast_convert_fusion.2
  372.6 4.5 convolution_convert_fusion.2
  377.1 4.6 reshape.143
  388.1 5.0 copy.49
  403.0 6.4 copy.48
  409.4 5.3 bitcast_convert_fusion.2
  425.8 4.6 reshape.143
  436.9 5.0 copy.49
  451.8 6.4 copy.48
  458.2 5.3 bitcast_convert_fusion.2
  470.1 4.5 convolution_convert_fusion.2
  474.6 4.6 reshape.143
  485.7 5.0 copy.49
  500.6 6.4 copy.48
  506.9 5.3 bitcast_convert_fusion.2
  523.4 4.6 reshape.143
  534.4 5.0 copy.49
  549.4 6.4 copy.48
  555.7 5.3 bitcast_convert_fusion.2
  567.7 4.5 convolution_convert_fusion.2
  572.2 4.6 reshape.143
  583.2 5.0 copy.49
  598.1 6.4 copy.48
  604.5 5.3 bitcast_convert_fusion.2
  620.9 4.6 reshape.143
  632.0 5.0 copy.49
  641.2 34.3 %scatter_custom_fusion = f32[2304,256]{1,0:T(8,128)S(1)} fusion(s32[6144]{0:T(1024)S(1)} %reshape.116, f32[6144,256]{1,0:T(8,128)} %bitcast.132, f32[]{:T(128)} %constant.4.clone.1), kind=kCustom, calls=%fused_computation.44 | custom fusion | flops 1572864 | bytes 2359808 | tf_op jit(solution)/shard_map/scatter-add | solution.py:109
  677.0 8.9 %collective-permute-done.4 = f32[3,256,256]{2,1,0:T(8,128)S(1)} collective-permute-done((f32[3,256,256]{2,1,0:T(8,128)S(1)}, f32[3,256,256]{2,1,0:T(8,128)S(1)}, u32[]{:S(2)}, u32[]{:S(2)}) %collective-permute-start.4) | collective-permute-done | bytes 786464 | tf_op jit(solution)/shard_map/ppermute | solution.py:29
  688.9 4.8 collective-permute-start.7
  693.9 5.2 collective-permute-done.6
  701.6 9.5 %all-to-all-start = ((f32[128,4,256]{2,1,0:T(4,128)}), f32[128,4,256]{2,1,0:T(4,128)S(1)}, u32[]{:S(2)}, u32[]{:S(2)}) async-start(f32[128,4,256]{2,1,0:T(4,128)} %reshape.105), calls=%async_computation | async-start | bytes 1048576 | tf_op jit(solution)/shard_map/all_to_all | solution.py:134
  711.8 13.5 %all-to-all-done = f32[128,4,256]{2,1,0:T(4,128)S(1)} async-done(((f32[128,4,256]{2,1,0:T(4,128)}), f32[128,4,256]{2,1,0:T(4,128)S(1)}, u32[]{:S(2)}, u32[]{:S(2)}) %all-to-all-start) | async-done | bytes 524320 | tf_op jit(solution)/shard_map/all_to_all | solution.py:134
  (149 shorter events, 228.6 us)
Async XLA Ops:
  0.6 5.0 collective-permute-start
  3.3 4.6 collective-permute-start.1
  7.9 185.8 %collective-permute-start.2 = (bf16[3,1,256,256]{3,2,1,0:T(8,128)(2,1)S(1)}, bf16[3,1,256,256]{3,2,1,0:T(8,128)(2,1)S(1)}, u32[]{:S(2)}, u32[]{:S(2)}) collective-permute-start(bf16[3,1,256,256]{3,2,1,0:T(8,128)(2,1)S(1)} %constant_dynamic-update-slice_fusion.1), channel_id=1, source_target_pairs={{0,1},{1,2},{2,3},{3,4},{4,5},{5,6},{6,7},{7,8},{8,9},{9,10},{10,1... | collective-permute-start | bytes 1179656 | tf_op jit(solution)/shard_map/ppermute | solution.py:18
  9.2 184.5 %collective-permute-start.3 = (bf16[3,1,256,256]{3,2,1,0:T(8,128)(2,1)S(1)}, bf16[3,1,256,256]{3,2,1,0:T(8,128)(2,1)S(1)}, u32[]{:S(2)}, u32[]{:S(2)}) collective-permute-start(bf16[3,1,256,256]{3,2,1,0:T(8,128)(2,1)S(1)} %constant_dynamic-update-slice_fusion.1), channel_id=1, source_target_pairs={{1,0},{2,1},{3,2},{4,3},{5,4},{6,5},{7,6},{8,7},{9,8},{10,9},{11,1... | collective-permute-start | bytes 1179656 | tf_op jit(solution)/shard_map/ppermute | solution.py:21
  222.1 28.4 %copy-start = (bf16[256,256]{1,0:T(8,128)(2,1)S(1)}, bf16[256,256]{1,0:T(8,128)(2,1)}, u32[]{:S(2)}) copy-start(bf16[256,256]{1,0:T(8,128)(2,1)} %param.18) | copy-start | bytes 393220
  222.1 28.4 %copy-start.1 = (bf16[256,256]{1,0:T(8,128)(2,1)S(1)}, bf16[256,256]{1,0:T(8,128)(2,1)}, u32[]{:S(2)}) copy-start(bf16[256,256]{1,0:T(8,128)(2,1)} %param.20) | copy-start | bytes 393220
  222.1 28.4 %copy-start.2 = (f32[256]{0:T(256)S(1)}, f32[256]{0:T(256)}, u32[]{:S(2)}) copy-start(f32[256]{0:T(256)} %param.22) | copy-start | bytes 3076
  222.1 28.3 %copy-start.3 = (f32[256]{0:T(256)S(1)}, f32[256]{0:T(256)}, u32[]{:S(2)}) copy-start(f32[256]{0:T(256)} %param.17) | copy-start | bytes 3076
  222.2 28.3 %copy-start.4 = (f32[256]{0:T(256)S(1)}, f32[256]{0:T(256)}, u32[]{:S(2)}) copy-start(f32[256]{0:T(256)} %param.19) | copy-start | bytes 3076
  222.2 28.3 %copy-start.5 = (f32[256]{0:T(256)S(1)}, f32[256]{0:T(256)}, u32[]{:S(2)}) copy-start(f32[256]{0:T(256)} %param.21) | copy-start | bytes 3076
  675.7 18.0 %copy-start.6 = (s32[1,1,256,1]{2,3,1,0:T(1,128)S(1)}, s32[1,1,256,1]{2,3,1,0:T(1,128)}, u32[]{:S(2)}) copy-start(s32[1,1,256,1]{2,3,1,0:T(1,128)} %param.23) | copy-start | bytes 3076
  675.7 10.2 %collective-permute-start.4 = (f32[3,256,256]{2,1,0:T(8,128)S(1)}, f32[3,256,256]{2,1,0:T(8,128)S(1)}, u32[]{:S(2)}, u32[]{:S(2)}) collective-permute-start(f32[3,256,256]{2,1,0:T(8,128)S(1)} %bitcast.127), channel_id=1, source_target_pairs={{0,16},{16,32},{32,48},{48,64},{64,80},{80,96},{96,112},{112,0},{1... | collective-permute-start | bytes 2359304 | tf_op jit(solution)/shard_map/ppermute | solution.py:29
  676.9 11.7 %collective-permute-start.5 = (f32[3,256,256]{2,1,0:T(8,128)S(1)}, f32[3,256,256]{2,1,0:T(8,128)S(1)}, u32[]{:S(2)}, u32[]{:S(2)}) collective-permute-start(f32[3,256,256]{2,1,0:T(8,128)S(1)} %bitcast.126), channel_id=1, source_target_pairs={{0,112},{16,0},{32,16},{48,32},{64,48},{80,64},{96,80},{112,96},{1... | collective-permute-start | bytes 2359304 | tf_op jit(solution)/shard_map/ppermute | solution.py:29
  688.9 10.3 %collective-permute-start.6 = (f32[256,256]{1,0:T(8,128)S(1)}, f32[256,256]{1,0:T(8,128)S(1)}, u32[]{:S(2)}, u32[]{:S(2)}) collective-permute-start(f32[256,256]{1,0:T(8,128)S(1)} %get-tuple-element.144), channel_id=1, source_target_pairs={{0,1},{1,2},{2,3},{3,4},{4,5},{5,6},{6,7},{7,8},{8,9},{9,10},{10,1... | collective-permute-start | bytes 786440 | tf_op jit(solution)/shard_map/ppermute | solution.py:29
  688.9 10.2 %collective-permute-start.7 = (f32[256,256]{1,0:T(8,128)S(1)}, f32[256,256]{1,0:T(8,128)S(1)}, u32[]{:S(2)}, u32[]{:S(2)}) collective-permute-start(f32[256,256]{1,0:T(8,128)S(1)} %get-tuple-element.145), channel_id=1, source_target_pairs={{0,15},{1,0},{2,1},{3,2},{4,3},{5,4},{6,5},{7,6},{8,7},{9,8},{10,9... | collective-permute-start | bytes 786440 | tf_op jit(solution)/shard_map/ppermute | solution.py:29
  701.6 23.7 %all-to-all-start = ((f32[128,4,256]{2,1,0:T(4,128)}), f32[128,4,256]{2,1,0:T(4,128)S(1)}, u32[]{:S(2)}, u32[]{:S(2)}) async-start(f32[128,4,256]{2,1,0:T(4,128)} %reshape.105), calls=%async_computation | async-start | bytes 1048576 | tf_op jit(solution)/shard_map/all_to_all | solution.py:134
where the time goes:
time: 734 us; the launch traced here: 726 us
  local copies, waits for them, and re-layouts  470 us (64%)
  matrix products  160 us (22%)
  other arithmetic  37.1 us (5%)
  waiting for transfers between devices  33.2 us (5%)
  starting transfers between devices  24.5 us (3%)
    dynamic_slice x24, local copies, waits for them, and re-layouts, on_device(): energy, pair_blocks = lax.map(group_work, (gathered, projector_all))  97.9 us
    while x1, local copies, waits for them, and re-layouts, on_device(): energy, pair_blocks = lax.map(group_work, (gathered, projector_all))  80.2 us
    reshape x1, local copies, waits for them, and re-layouts, on_device(): correlations.reshape(group_count, group, projectors, neighbour_count, orb...  74.6 us
    dot_general x8, matrix products, group_work(): jnp.einsum('apkq,arkq->apr', partial_value, projector, preferred_element_...  42.1 us
    dot_general x8, local copies, waits for them, and re-layouts, group_work(): jnp.einsum('apko,apkq->akoq', projector, lifted, preferred_element_type=j...  40.1 us
    reshape x8, local copies, waits for them, and re-layouts, group_work(): slope = slope.reshape(group, projectors, projectors)  36.4 us
    dot_general x8, matrix products, group_work(): jnp.dot(grad_first, weight_first.T, preferred_element_type=jnp.float32)  35.9 us
    dot_general x8, matrix products, group_work(): jnp.einsum('apko,apkq->akoq', projector, lifted, preferred_element_type=j...  35.2 us
  transfers between devices with their start and end apart: 9, of which 6 were waited for; matrix products, arithmetic and copies ran while one was open for 25% of the time, Pallas kernels for 0%

commit v1 on v0

v1 whole, which is shorter than its diff:
```python
import functools
import jax, jax.numpy as jnp
from jax import lax
from jax.experimental import pallas as pl
from jax.experimental.pallas import tpu as pltpu
from jax.sharding import PartitionSpec as P
F32, BF = jnp.float32, jnp.bfloat16
NP, NK, NO, H, A = 90, 24, 16, 256, 256
PR = 96
G = 16
NT = (((1,), (1,)), ((), ()))

def dot(a, b):
    return jnp.dot(a, b, preferred_element_type=F32)
def dot_nt(a, b):
    return lax.dot_general(a, b, NT, preferred_element_type=F32)

def diag(x, y):
    z = jnp.zeros_like(x)
    return jnp.concatenate([jnp.concatenate([x, z], 1), jnp.concatenate([z, y], 1)], 0)

def k1_body(unroll, nbr, ext, sel, corr, mask, d_ref, ot_ref, table, tmp):
    step = pl.program_id(0)
    @pl.when(step == 0)
    def _():
        tmp[pl.ds(270 * 16, 18 * 16), :] = jnp.zeros((18 * 16, 128), F32)
        @pl.loop(0, 9)
        def _(b):
            for o in range(16):
                t = dot(ext[pl.ds(pl.multiple_of(b * 256, 256), 256), :], sel[:, o * 128:(o + 1) * 128])
                tmp[pl.ds(o, 256, stride=16), :] = t
            table[pl.ds(b * 256, 256)] = tmp[pl.ds(0, 4096), :].reshape(256, 16, 128).astype(BF)
    @pl.loop(0, 10)
    def _(c):
        for r in range(27):
            x = corr[:, pl.ds(pl.multiple_of((c * 27 + r) * 128, 128), 128)].astype(F32)
            tmp[pl.ds(pl.multiple_of((c * 27 + r) * 16, 16), 16), :] = x
    eye = (lax.broadcasted_iota(jnp.int32, (128, 256), 0) == lax.broadcasted_iota(jnp.int32, (128, 256), 1) % 128).astype(BF)
    pad = jnp.zeros((128 - PR, 128), BF)
    d2 = d_ref.reshape(PR * G, 128)
    def pair(i):
        d = jnp.zeros((PR, 256), F32)
        for j in range(3):
            o = [tmp[pl.ds(j * 16 + 2 * i + h, PR, stride=48), :].astype(BF) for h in range(2)]
            bd = []
            for h in range(2):
                base = (step * G + 2 * i + h) * NK + 8 * j
                bd.append(jnp.concatenate([table[nbr[base + kk]] * mask[kk] for kk in range(8)], 0))
            p = dot(jnp.concatenate(o, 1), diag(*bd)).astype(BF)
            rhs = diag(*[jnp.concatenate([v, pad], 0) for v in o])
            r = dot_nt(jnp.concatenate([p, eye], 0), rhs)
            d = d + r[:PR]
            ot_ref[i, j * 128:(j + 1) * 128, :] = r[PR:].astype(BF)
        for h in range(2):
            d2[pl.ds(2 * i + h, PR, stride=G), :] = d[:, h * 128:(h + 1) * 128]
    @pl.loop(0, G // 2 // unroll)
    def _(i):
        for u in range(unroll):
            pair(i * unroll + u)

def k1(nbr, ext, sel, corr, mask, unroll=1):
    return pl.pallas_call(
        functools.partial(k1_body, unroll),
        grid_spec=pltpu.PrefetchScalarGridSpec(
            num_scalar_prefetch=1, grid=(A // G,),
            in_specs=[pl.BlockSpec((9 * A, 256), lambda s, n: (0, 0)),
                      pl.BlockSpec((256, 2048), lambda s, n: (0, 0)),
                      pl.BlockSpec((G, 34560), lambda s, n: (s, 0)),
                      pl.BlockSpec((8, 16, 128), lambda s, n: (0, 0, 0))],
            out_specs=[pl.BlockSpec((PR, G, 128), lambda s, n: (0, s, 0)),
                       pl.BlockSpec((G // 2, 384, 256), lambda s, n: (s, 0, 0))],
            scratch_shapes=[pltpu.VMEM((9 * A, 16, 128), BF), pltpu.VMEM((288 * 16, 128), F32)]),
        out_shape=[jax.ShapeDtypeStruct((PR, A, 128), F32), jax.ShapeDtypeStruct((A // 2, 384, 256), BF)],
        compiler_params=pltpu.CompilerParams(vmem_limit_bytes=60 << 20, dimension_semantics=("arbitrary",)),
        name="descriptor",
    )(nbr, ext, sel, corr, mask)

def consts():
    i = jnp.arange(256)[:, None]; c = jnp.arange(2048)[None]
    sel = ((i // 16 == c // 128) & (i % 16 == c % 16)).astype(BF)
    k = jnp.arange(8)[:, None, None]; l = jnp.arange(128)[None, None]
    mask = jnp.broadcast_to((l // 16 == k), (8, 16, 128)).astype(BF)
    return sel, mask

def relay(corr):
    return corr.reshape(256, 34560)

PC = 16
def k2_body(d_ref, w1, b1, w2, b2, w3, b3, ro, e_ref, s_ref, acc, grad):
    phase, c = pl.program_id(0), pl.program_id(1)
    last = pl.num_programs(1) - 1
    @pl.when(phase == 0)
    def _():
        t = jnp.zeros((A, H), F32)
        for p in range(0, PC, 2):
            x = jnp.concatenate([d_ref[p], d_ref[p + 1]], 1).astype(BF)
            t = t + dot(x, w1[p:p + 2].reshape(256, H))
        acc[...] = jnp.where(c == 0, 0.0, acc[...]) + t
        @pl.when(c == last)
        def _():
            act1 = jnp.tanh(acc[...] + b1[...])
            th2 = jnp.tanh(dot(act1.astype(BF), w2[...]) + b2[...])
            act2 = act1 + th2
            th3 = jnp.tanh(dot(act2.astype(BF), w3[...]) + b3[...])
            e_ref[...] = jnp.sum((act2 + th3) * ro[...], axis=1, keepdims=True)
            g3 = (ro[...] * (1.0 - th3 * th3)).astype(BF)
            back2 = ro[...] + dot_nt(g3, w3[...])
            g2 = (back2 * (1.0 - th2 * th2)).astype(BF)
            back1 = back2 + dot_nt(g2, w2[...])
            grad[...] = (back1 * (1.0 - act1 * act1)).astype(BF)
    @pl.when(phase == 1)
    def _():
        for p in range(0, PC, 2):
            t = dot_nt(grad[...], w1[p:p + 2].reshape(256, H))
            s_ref[p] = t[:, :128]
            s_ref[p + 1] = t[:, 128:]

def k2(d, w1p, b1, w2, b2, w3, b3, ro):
    n = PR // PC
    row = lambda: pl.BlockSpec((1, H), lambda f, c: (0, 0))
    mat = lambda: pl.BlockSpec((H, H), lambda f, c: (0, 0))
    return pl.pallas_call(
        k2_body, grid=(2, n),
        in_specs=[pl.BlockSpec((PC, A, 128), lambda f, c: (jnp.where(f == 0, c, n - 1), 0, 0)),
                  pl.BlockSpec((PC, 128, H), lambda f, c: (c, 0, 0)),
                  row(), mat(), row(), mat(), row(), row()],
        out_specs=[pl.BlockSpec((A, 1), lambda f, c: (0, 0)),
                   pl.BlockSpec((PC, A, 128), lambda f, c: (jnp.where(f == 0, 0, c), 0, 0))],
        scratch_shapes=[pltpu.VMEM((A, H), F32), pltpu.VMEM((A, H), BF)],
        out_shape=[jax.ShapeDtypeStruct((A, 1), F32), jax.ShapeDtypeStruct((PR, A, 128), F32)],
        compiler_params=pltpu.CompilerParams(vmem_limit_bytes=40 << 20),
        name="network",
    )(d, w1p, b1, w2, b2, w3, b3, ro)

def k3_body(unroll, nbr, s_ref, ot_ref, fold, out_ref, acc, lift):
    step = pl.program_id(0)
    @pl.when(step == 0)
    def _():
        @pl.loop(0, 144)
        def _(c):
            acc[pl.ds(c * 16, 16)] = jnp.zeros((16, 16, 128), F32)
    s2 = s_ref.reshape(PR * G, 128)
    pad = jnp.zeros((128 - PR, 128), BF)
    lane = lax.broadcasted_iota(jnp.int32, (16, 128), 1) // 16
    def pair(i):
        s = [jnp.concatenate([s2[pl.ds(2 * i + h, PR, stride=G), :].astype(BF), pad], 0) for h in range(2)]
        lt = dot_nt(ot_ref[i], diag(*s)).astype(BF)
        for j in range(3):
            ot = ot_ref[i, j * 128:(j + 1) * 128, :]
            zero = jnp.zeros((128, 128), BF)
            rhs = jnp.concatenate([jnp.concatenate([ot[:, :128], zero], 1), jnp.concatenate([zero, ot[:, 128:]], 1)], 0)
            r = dot_nt(lt[j * 128:(j + 1) * 128], rhs)
            for h in range(2):
                base = (step * G + 2 * i + h) * NK + 8 * j
                ns = [nbr[base + kk] for kk in range(8)]
                new = [acc[ns[kk]] + r[kk * 16:(kk + 1) * 16, h * 128:(h + 1) * 128] for kk in range(8)]
                for kk in range(8):
                    pltpu.store(acc.at[ns[kk]], new[kk], mask=lane == kk)
    @pl.loop(0, G // 2 // unroll)
    def _(i):
        for u in range(unroll):
            pair(i * unroll + u)
    @pl.when(step == pl.num_programs(0) - 1)
    def _():
        acc2 = acc.reshape(9 * A * 16, 128)
        @pl.loop(0, 9)
        def _(b):
            t = jnp.zeros((256, 256), F32)
            for q in range(0, 16, 2):
                x = jnp.concatenate([acc2[pl.ds(b * 4096 + q + h, 256, stride=16), :] for h in range(2)], 1).astype(BF)
                t = t + dot(x, fold[q * 128:(q + 2) * 128, :])
            out_ref[pl.ds(pl.multiple_of(b * 256, 256), 256), :] = t.astype(BF)

def k3(nbr, s, ot, fold, unroll=1):
    return pl.pallas_call(
        functools.partial(k3_body, unroll),
        grid_spec=pltpu.PrefetchScalarGridSpec(
            num_scalar_prefetch=1, grid=(A // G,),
            in_specs=[pl.BlockSpec((PR, G, 128), lambda s, n: (0, s, 0)),
                      pl.BlockSpec((G // 2, 384, 256), lambda s, n: (s, 0, 0)),
                      pl.BlockSpec((2048, 256), lambda s, n: (0, 0))],
            out_specs=pl.BlockSpec((9 * A, 256), lambda s, n: (0, 0)),
            scratch_shapes=[pltpu.VMEM((9 * A, 16, 128), F32), pltpu.VMEM((384, 256), BF)]),
        out_shape=jax.ShapeDtypeStruct((9 * A, 256), BF),
        compiler_params=pltpu.CompilerParams(vmem_limit_bytes=60 << 20),
        name="hamilton",
    )(nbr, s, ot, fold)

def fold_of():
    i = jnp.arange(2048)[:, None]; c = jnp.arange(256)[None]
    return ((i // 128 == c % 16) & (i % 16 == c // 16)).astype(BF)

def w1_of(w):
    return jnp.pad(w.reshape(NP, NP, H), ((0, PR - NP), (0, 128 - NP), (0, 0)))


def shifted(value, axis, steps):
    count = lax.axis_size(axis)
    return lax.ppermute(value, axis, [(s, (s + steps) % count) for s in range(count)])


def padded(block, sides):
    for axis, dim in sides:
        block = jnp.concatenate([shifted(block, axis, 1), block, shifted(block, axis, -1)], axis=dim)
    return block


def on_device(density, neighbours, correlations, weight_first, bias_first, weight_second, bias_second,
              weight_third, bias_third, readout, destination):
    sel, mask = consts()
    nbr = neighbours.reshape(A * NK)
    ext = padded(density, (("gy", 1), ("gx", 0))).reshape(9 * A, 256)
    row = lambda v: v.reshape(1, H)
    d, ot = k1(nbr, ext, sel, relay(correlations), mask, 4)
    energy, slope = k2(d, w1_of(weight_first), row(bias_first), weight_second, row(bias_second),
                       weight_third, row(bias_third), row(readout))
    part = k3(nbr, slope, ot, fold_of(), 1).reshape(3, 3, A, 256)
    folded = part[1].astype(F32)
    for s in (1, -1):
        folded = folded + shifted(part[1 + s], "gx", s).astype(F32)
    hamilton = folded[1]
    for s in (1, -1):
        hamilton = hamilton + shifted(folded[1 + s].astype(BF), "gy", s).astype(F32)
    target = destination.reshape(A)
    order = jnp.arange(A, dtype=jnp.int32)
    earlier = (target[:, None] == target[None, :]) & (order[None, :] < order[:, None])
    position = target * 4 + jnp.sum(earlier.astype(jnp.int32), axis=1)
    chosen = (jnp.arange(512, dtype=jnp.int32)[:, None] == position[None, :]).astype(BF)
    outgoing = dot(chosen, hamilton.astype(BF)).astype(BF).reshape(128, 4, 256)
    received = lax.all_to_all(outgoing, ("gx", "gy"), split_axis=0, concat_axis=0, tiled=True)
    return energy.reshape(1, 1, A), received[None].astype(F32)


def solution(mesh):
    own = P("gx", "gy", None, None)
    return jax.shard_map(
        on_device,
        mesh=mesh,
        in_specs=(own, own, own, P(), P(), P(), P(), P(), P(), P(), own),
        out_specs=(P("gx", "gy", None), P(("gx", "gy"), None, None, None)),
        check_vma=False,
    )
```

time: 734 us -> 220 us (0.30)
  local copies, waits for them, and re-layouts: 470 us -> 19.7 us
  matrix products: 160 us -> 0.26 us
  Pallas kernels: 0 us -> 142 us
  other arithmetic: 37.1 us -> 6.73 us
  waiting for transfers between devices: 33.2 us -> 24.8 us
    reshape x19 -> x3, local copies, waits for them, and re-layouts: 164 us -> 8.38 us  [the longest x1 6.89 us: w1_of(): return jnp.pad(w.reshape(NP, NP, H), ((0, PR - NP), (0, 128 - NP), (0, 0)))]
    dot_general x56 -> x1, matrix products: 143 us -> 0.26 us  [dot(): return jnp.dot(a, b, preferred_element_type=F32)]
    pallas_call x0 -> x3, Pallas kernels: none -> 142 us  [the longest x1 69.3 us: k3(): pl.pallas_call(functools.partial(k3_body, unroll), grid_spec=pltpu.Prefet...]
    dynamic_slice x24 -> x0, local copies, waits for them, and re-layouts: 97.9 us -> none  [on_device(): energy, pair_blocks = lax.map(group_work, (gathered, projector_all))]
    while x1 -> x0, local copies, waits for them, and re-layouts: 80.2 us -> none  [on_device(): energy, pair_blocks = lax.map(group_work, (gathered, projector_all))]
    dot_general x8 -> x0, local copies, waits for them, and re-layouts: 40.1 us -> none  [group_work(): jnp.einsum('apko,apkq->akoq', projector, lifted, preferred_element_type=j...]
    scatter-add x1 -> x0, other arithmetic: 34.3 us -> none  [on_device(): jax.ops.segment_sum(pair_blocks.reshape(atom_count * neighbour_count, blo...]
    dynamic_update_slice x24 -> x0, local copies, waits for them, and re-layouts: 32.1 us -> none  [on_device(): energy, pair_blocks = lax.map(group_work, (gathered, projector_all))]
  transfers between devices with their start and end apart: 9 -> 9, of which waited for: 6 -> 6; matrix products, arithmetic and copies ran while one was open for 25% -> 9% of each run, Pallas kernels for 0% -> 0%
where the time goes in v1:
time: 220 us; the launch traced here: 219 us
  Pallas kernels  142 us (65%)
  waiting for transfers between devices  24.8 us (11%)
  starting transfers between devices  24.1 us (11%)
  local copies, waits for them, and re-layouts  19.7 us (9%)
  other arithmetic  6.73 us (3%)
    pallas_call x1, Pallas kernels, k3(): pl.pallas_call(functools.partial(k3_body, unroll), grid_spec=pltpu.Prefet...  69.3 us
    pallas_call x1, Pallas kernels, k1(): pl.pallas_call(functools.partial(k1_body, unroll), grid_spec=pltpu.Prefet...  59.4 us
    ppermute x8, starting transfers between devices, shifted(): lax.ppermute(value, axis, [(s, (s + steps) % count) for s in range(count)])  14.4 us
    ppermute x8, waiting for transfers between devices, shifted(): lax.ppermute(value, axis, [(s, (s + steps) % count) for s in range(count)])  14 us
    pallas_call x1, Pallas kernels, k2(): pl.pallas_call(k2_body, grid=(2, n), in_specs=[pl.BlockSpec((PC, A, 128),...  13.8 us
    all_to_all x1, waiting for transfers between devices, on_device(): lax.all_to_all(outgoing, ('gx', 'gy'), split_axis=0, concat_axis=0, tiled...  10.8 us
    all_to_all x1, starting transfers between devices, on_device(): lax.all_to_all(outgoing, ('gx', 'gy'), split_axis=0, concat_axis=0, tiled...  9.68 us
    reshape x1, local copies, waits for them, and re-layouts, w1_of(): return jnp.pad(w.reshape(NP, NP, H), ((0, PR - NP), (0, 128 - NP), (0, 0)))  6.89 us
  transfers between devices with their start and end apart: 9, of which 6 were waited for; matrix products, arithmetic and copies ran while one was open for 9% of the time, Pallas kernels for 0%

profile of v1, /device:TPU:1, one launch (start us, length us, event | category | flops | bytes accessed | tf_op | source)
XLA Modules:
  0.0 218.9 jit_solution(5463990874476470880)
XLA Ops:
  0.6 2.1 collective-permute-start
  2.7 4.8 %collective-permute-start.1 = (bf16[1,1,256,256]{3,2,1,0:T(8,128)(2,1)}, bf16[1,1,256,256]{3,2,1,0:T(8,128)(2,1)S(1)}, u32[]{:S(2)}, u32[]{:S(2)}) collective-permute-start(bf16[1,1,256,256]{3,2,1,0:T(8,128)(2,1)} %param.11), channel_id=1, source_target_pairs={{0,15},{1,0},{2,1},{3,2},{4,3},{5,4},{6,5},{7,6},{8,7},{9,8},{10,9... | collective-permute-start | bytes 393224 | tf_op jit(solution)/shard_map/ppermute | solution.py:199
  7.6 0.8 copy.14
  8.4 0.7 reshape.327.nbr
  9.1 6.9 %reshape.330 = bf16[90,90,256]{2,1,0:T(8,128)(2,1)} reshape(bf16[8100,256]{1,0:T(8,128)(2,1)} %param.14) | data formatting | bytes 8294400 | tf_op jit(solution)/shard_map/reshape | solution.py:194
  16.0 5.7 %pad.4.w1 = bf16[96,128,256]{2,1,0:T(8,128)(2,1)} pad(bf16[90,90,256]{2,1,0:T(8,128)(2,1)} %reshape.330, bf16[]{:T(256)} %constant.109.clone.1), padding=0_6x0_38x0_0 | pad | bytes 10438658 | tf_op jit(solution)/shard_map/jit(_pad)/pad | solution.py:194
  21.7 1.4 and_convert_fusion.1.sel
  23.1 0.0 collective-permute-done
  23.1 0.0 copy-done.7
  23.2 0.0 collective-permute-done.1
  23.2 2.1 collective-permute-start.2
  25.3 0.0 collective-permute-start.3
  25.3 2.4 %and_convert_fusion.fold = bf16[2048,256]{1,0:T(8,128)(2,1)} fusion(s32[256]{0:T(256)S(1)} %get-tuple-element.20, s32[256]{0:T(256)S(1)} %get-tuple-element.19, s32[2048]{0:T(1024)S(1)} %get-tuple-element.17, s32[2048]{0:T(1024)S(1)} %get-tuple-element.18), kind=kLoop, calls=%fused_computation | loop fusion | flops 2097152 | bytes 1067008 | tf_op jit(solution)/shard_map/convert_element_type | solution.py:191
  27.7 2.4 %collective-permute-done.2 = bf16[1,3,256,256]{3,2,1,0:T(8,128)(2,1)S(1)} collective-permute-done((bf16[1,3,256,256]{3,2,1,0:T(8,128)(2,1)S(1)}, bf16[1,3,256,256]{3,2,1,0:T(8,128)(2,1)S(1)}, u32[]{:S(2)}, u32[]{:S(2)}) %collective-permute-start.2) | collective-permute-done | bytes 393248 | tf_op jit(solution)/shard_map/ppermute | solution.py:199
  30.1 2.5 %collective-permute-done.3 = bf16[1,3,256,256]{3,2,1,0:T(8,128)(2,1)S(1)} collective-permute-done((bf16[1,3,256,256]{3,2,1,0:T(8,128)(2,1)S(1)}, bf16[1,3,256,256]{3,2,1,0:T(8,128)(2,1)S(1)}, u32[]{:S(2)}, u32[]{:S(2)}) %collective-permute-start.3) | collective-permute-done | bytes 393248 | tf_op jit(solution)/shard_map/ppermute | solution.py:199
  32.5 1.1 pad_maximum_fusion
  33.7 0.6 broadcast_in_dim.2.mask
  34.3 0.0 copy-start.5
  34.3 0.0 copy-start.6
  34.3 59.4 %descriptor.1 = (f32[96,256,128]{2,1,0:T(8,128)}, bf16[128,384,256]{2,1,0:T(8,128)(2,1)}) custom-call(s32[6144]{0:T(1024)} %reshape.327.nbr, bf16[2304,256]{1,0:T(8,128)(2,1)} %bitcast.35, bf16[256,2048]{1,0:T(8,128)(2,1)} %and_convert_fusion.1.sel, bf16[256,34560]{1,0:T(8,128)(2,1)} %bitcast.34, bf16[8,16,128]{2,1,0:T(8,128)(2,1)} %broadcast_in_dim.2.mask), custom_call_target="tpu_custom_call" | custom-call | tf_op jit(solution)/shard_map/descriptor/pallas_call | solution.py:62
  93.7 0.0 copy-done.1
  93.7 0.0 copy-done.2
  93.7 0.0 copy-done.3
  93.7 0.0 copy-done.4
  93.7 0.0 copy-done.5
  93.8 0.0 copy-done.6
  93.8 0.0 copy-start
  93.8 2.8 %copy-done = bf16[96,128,256]{2,1,0:T(8,128)(2,1)S(1)} copy-done((bf16[96,128,256]{2,1,0:T(8,128)(2,1)S(1)}, bf16[96,128,256]{2,1,0:T(8,128)(2,1)}, u32[]{:S(2)}) %copy-start) | copy-done | bytes 6291480
  96.6 13.8 %network.1 = (f32[256,1]{1,0:T(8,128)S(1)}, f32[96,256,128]{2,1,0:T(8,128)}) custom-call(f32[96,256,128]{2,1,0:T(8,128)} %get-tuple-element.6.d_ref, bf16[96,128,256]{2,1,0:T(8,128)(2,1)S(1)} %copy-done, f32[1,256]{1,0:T(1,128)S(1)} %bitcast.30, bf16[256,256]{1,0:T(8,128)(2,1)S(1)} %copy-done.1, f32[1,256]{1,0:T(1,128)S(1)} %bitcast.31, ...), custom_call_target="tpu_custom_call" | custom-call | tf_op jit(solution)/shard_map/network/pallas_call | solution.py:122
  110.3 69.3 %hamilton.1 = bf16[2304,256]{1,0:T(8,128)(2,1)} custom-call(s32[6144]{0:T(1024)} %reshape.327.nbr, f32[96,256,128]{2,1,0:T(8,128)} %get-tuple-element.8.s_ref, bf16[128,384,256]{2,1,0:T(8,128)(2,1)} %get-tuple-element.9.ot_ref, bf16[2048,256]{1,0:T(8,128)(2,1)} %and_convert_fusion.fold), custom_call_target="tpu_custom_call" | custom-call | tf_op jit(solution)/shard_map/hamilton/pallas_call | solution.py:175
  179.7 1.3 fusion.18
  181.0 0.0 collective-permute-start.4
  181.0 0.5 collective-permute-start.5
  181.5 0.0 copy-done.8
  181.5 0.2 convert_reduce_fusion
  181.7 4.0 %collective-permute-done.4 = bf16[3,256,256]{2,1,0:T(8,128)(2,1)S(1)} collective-permute-done((bf16[3,256,256]{2,1,0:T(8,128)(2,1)S(1)}, bf16[3,256,256]{2,1,0:T(8,128)(2,1)S(1)}, u32[]{:S(2)}, u32[]{:S(2)}) %collective-permute-start.4) | collective-permute-done | bytes 393248 | tf_op jit(solution)/shard_map/ppermute | solution.py:199
  185.7 2.8 %collective-permute-done.5 = bf16[3,256,256]{2,1,0:T(8,128)(2,1)S(1)} collective-permute-done((bf16[3,256,256]{2,1,0:T(8,128)(2,1)S(1)}, bf16[3,256,256]{2,1,0:T(8,128)(2,1)S(1)}, u32[]{:S(2)}, u32[]{:S(2)}) %collective-permute-start.5) | collective-permute-done | bytes 393248 | tf_op jit(solution)/shard_map/ppermute | solution.py:199
  188.5 0.1 fusion.16
  188.7 0.1 collective-permute-start.6
  188.8 4.8 %collective-permute-start.7 = (bf16[256,256]{1,0:T(8,128)(2,1)S(1)}, bf16[256,256]{1,0:T(8,128)(2,1)S(1)}, u32[]{:S(2)}, u32[]{:S(2)}) collective-permute-start(bf16[256,256]{1,0:T(8,128)(2,1)S(1)} %get-tuple-element.16), channel_id=1, source_target_pairs={{0,15},{1,0},{2,1},{3,2},{4,3},{5,4},{6,5},{7,6},{8,7},{9,8},{10,9... | collective-permute-start | bytes 393224 | tf_op jit(solution)/shard_map/ppermute | solution.py:199
  193.5 2.3 %collective-permute-done.6 = bf16[256,256]{1,0:T(8,128)(2,1)S(1)} collective-permute-done((bf16[256,256]{1,0:T(8,128)(2,1)S(1)}, bf16[256,256]{1,0:T(8,128)(2,1)S(1)}, u32[]{:S(2)}, u32[]{:S(2)}) %collective-permute-start.6) | collective-permute-done | bytes 131104 | tf_op jit(solution)/shard_map/ppermute | solution.py:199
  195.9 0.0 collective-permute-done.7
  195.9 0.3 convolution_convert_fusion
  196.2 0.8 reshape.337
  196.9 9.7 %all-to-all-start = ((bf16[128,4,256]{2,1,0:T(4,128)(2,1)}), bf16[128,4,256]{2,1,0:T(4,128)(2,1)S(1)}, u32[]{:S(2)}, u32[]{:S(2)}) async-start(bf16[128,4,256]{2,1,0:T(4,128)(2,1)} %reshape.337), calls=%async_computation | async-start | bytes 524288 | tf_op jit(solution)/shard_map/all_to_all | solution.py:230
  206.6 0.7 reduce
  207.3 10.8 %all-to-all-done = bf16[128,4,256]{2,1,0:T(4,128)(2,1)S(1)} async-done(((bf16[128,4,256]{2,1,0:T(4,128)(2,1)}), bf16[128,4,256]{2,1,0:T(4,128)(2,1)S(1)}, u32[]{:S(2)}, u32[]{:S(2)}) %all-to-all-start) | async-done | bytes 262176 | tf_op jit(solution)/shard_map/all_to_all | solution.py:230
  218.1 0.9 bitcast_convert_fusion
  (15 shorter events, 0.1 us)
Async XLA Ops:
  0.6 22.5 %collective-permute-start = (bf16[1,1,256,256]{3,2,1,0:T(8,128)(2,1)}, bf16[1,1,256,256]{3,2,1,0:T(8,128)(2,1)S(1)}, u32[]{:S(2)}, u32[]{:S(2)}) collective-permute-start(bf16[1,1,256,256]{3,2,1,0:T(8,128)(2,1)} %param.11), channel_id=1, source_target_pairs={{0,1},{1,2},{2,3},{3,4},{4,5},{5,6},{6,7},{7,8},{8,9},{9,10},{10,1... | collective-permute-start | bytes 393224 | tf_op jit(solution)/shard_map/ppermute | solution.py:199
  2.7 20.4 %collective-permute-start.1 = (bf16[1,1,256,256]{3,2,1,0:T(8,128)(2,1)}, bf16[1,1,256,256]{3,2,1,0:T(8,128)(2,1)S(1)}, u32[]{:S(2)}, u32[]{:S(2)}) collective-permute-start(bf16[1,1,256,256]{3,2,1,0:T(8,128)(2,1)} %param.11), channel_id=1, source_target_pairs={{0,15},{1,0},{2,1},{3,2},{4,3},{5,4},{6,5},{7,6},{8,7},{9,8},{10,9... | collective-permute-start | bytes 393224 | tf_op jit(solution)/shard_map/ppermute | solution.py:199
  16.0 7.1 %copy-start.7 = (bf16[1,1,256,256]{3,2,1,0:T(8,128)(2,1)S(1)}, bf16[1,1,256,256]{3,2,1,0:T(8,128)(2,1)}, u32[]{:S(2)}) copy-start(bf16[1,1,256,256]{3,2,1,0:T(8,128)(2,1)} %param.11) | copy-start | bytes 393220
  23.2 6.9 %collective-permute-start.2 = (bf16[1,3,256,256]{3,2,1,0:T(8,128)(2,1)S(1)}, bf16[1,3,256,256]{3,2,1,0:T(8,128)(2,1)S(1)}, u32[]{:S(2)}, u32[]{:S(2)}) collective-permute-start(bf16[1,3,256,256]{3,2,1,0:T(8,128)(2,1)S(1)} %constant_dynamic-update-slice_fusion), channel_id=1, source_target_pairs={{0,16},{16,32},{32,48},{48,64},{64,80},{80,96},{96,112},{112,0},{1... | collective-permute-start | bytes 1179656 | tf_op jit(solution)/shard_map/ppermute | solution.py:199
  25.3 7.2 %collective-permute-start.3 = (bf16[1,3,256,256]{3,2,1,0:T(8,128)(2,1)S(1)}, bf16[1,3,256,256]{3,2,1,0:T(8,128)(2,1)S(1)}, u32[]{:S(2)}, u32[]{:S(2)}) collective-permute-start(bf16[1,3,256,256]{3,2,1,0:T(8,128)(2,1)S(1)} %constant_dynamic-update-slice_fusion), channel_id=1, source_target_pairs={{0,112},{16,0},{32,16},{48,32},{64,48},{80,64},{96,80},{112,96},{1... | collective-permute-start | bytes 1179656 | tf_op jit(solution)/shard_map/ppermute | solution.py:199
  34.3 59.4 %copy-start.1 = (bf16[256,256]{1,0:T(8,128)(2,1)S(1)}, bf16[256,256]{1,0:T(8,128)(2,1)}, u32[]{:S(2)}) copy-start(bf16[256,256]{1,0:T(8,128)(2,1)} %w2.1) | copy-start | bytes 393220
  34.3 59.4 %copy-start.2 = (bf16[256,256]{1,0:T(8,128)(2,1)S(1)}, bf16[256,256]{1,0:T(8,128)(2,1)}, u32[]{:S(2)}) copy-start(bf16[256,256]{1,0:T(8,128)(2,1)} %w3.1) | copy-start | bytes 393220
  34.3 59.4 %copy-start.3 = (f32[256]{0:T(256)S(1)}, f32[256]{0:T(256)}, u32[]{:S(2)}) copy-start(f32[256]{0:T(256)} %param.15) | copy-start | bytes 3076
  34.3 59.4 %copy-start.4 = (f32[256]{0:T(256)S(1)}, f32[256]{0:T(256)}, u32[]{:S(2)}) copy-start(f32[256]{0:T(256)} %param.17) | copy-start | bytes 3076
  34.3 59.4 %copy-start.5 = (f32[256]{0:T(256)S(1)}, f32[256]{0:T(256)}, u32[]{:S(2)}) copy-start(f32[256]{0:T(256)} %param.19) | copy-start | bytes 3076
  34.3 59.4 %copy-start.6 = (f32[256]{0:T(256)S(1)}, f32[256]{0:T(256)}, u32[]{:S(2)}) copy-start(f32[256]{0:T(256)} %param.20) | copy-start | bytes 3076
  93.8 2.8 %copy-start = (bf16[96,128,256]{2,1,0:T(8,128)(2,1)S(1)}, bf16[96,128,256]{2,1,0:T(8,128)(2,1)}, u32[]{:S(2)}) copy-start(bf16[96,128,256]{2,1,0:T(8,128)(2,1)} %pad.4.w1) | copy-start | bytes 18874372
  179.7 1.9 copy-start.8
  181.0 4.7 %collective-permute-start.4 = (bf16[3,256,256]{2,1,0:T(8,128)(2,1)S(1)}, bf16[3,256,256]{2,1,0:T(8,128)(2,1)S(1)}, u32[]{:S(2)}, u32[]{:S(2)}) collective-permute-start(bf16[3,256,256]{2,1,0:T(8,128)(2,1)S(1)} %bitcast.38), channel_id=1, source_target_pairs={{0,16},{16,32},{32,48},{48,64},{64,80},{80,96},{96,112},{112,0},{1... | collective-permute-start | bytes 1179656 | tf_op jit(solution)/shard_map/ppermute | solution.py:199
  181.0 7.5 %collective-permute-start.5 = (bf16[3,256,256]{2,1,0:T(8,128)(2,1)S(1)}, bf16[3,256,256]{2,1,0:T(8,128)(2,1)S(1)}, u32[]{:S(2)}, u32[]{:S(2)}) collective-permute-start(bf16[3,256,256]{2,1,0:T(8,128)(2,1)S(1)} %bitcast.37), channel_id=1, source_target_pairs={{0,112},{16,0},{32,16},{48,32},{64,48},{80,64},{96,80},{112,96},{1... | collective-permute-start | bytes 1179656 | tf_op jit(solution)/shard_map/ppermute | solution.py:199
  188.7 7.2 %collective-permute-start.6 = (bf16[256,256]{1,0:T(8,128)(2,1)S(1)}, bf16[256,256]{1,0:T(8,128)(2,1)S(1)}, u32[]{:S(2)}, u32[]{:S(2)}) collective-permute-start(bf16[256,256]{1,0:T(8,128)(2,1)S(1)} %get-tuple-element.15), channel_id=1, source_target_pairs={{0,1},{1,2},{2,3},{3,4},{4,5},{5,6},{6,7},{7,8},{8,9},{9,10},{10,1... | collective-permute-start | bytes 393224 | tf_op jit(solution)/shard_map/ppermute | solution.py:199
  188.8 7.1 %collective-permute-start.7 = (bf16[256,256]{1,0:T(8,128)(2,1)S(1)}, bf16[256,256]{1,0:T(8,128)(2,1)S(1)}, u32[]{:S(2)}, u32[]{:S(2)}) collective-permute-start(bf16[256,256]{1,0:T(8,128)(2,1)S(1)} %get-tuple-element.16), channel_id=1, source_target_pairs={{0,15},{1,0},{2,1},{3,2},{4,3},{5,4},{6,5},{7,6},{8,7},{9,8},{10,9... | collective-permute-start | bytes 393224 | tf_op jit(solution)/shard_map/ppermute | solution.py:199
  196.9 21.1 %all-to-all-start = ((bf16[128,4,256]{2,1,0:T(4,128)(2,1)}), bf16[128,4,256]{2,1,0:T(4,128)(2,1)S(1)}, u32[]{:S(2)}, u32[]{:S(2)}) async-start(bf16[128,4,256]{2,1,0:T(4,128)(2,1)} %reshape.337), calls=%async_computation | async-start | bytes 524288 | tf_op jit(solution)/shard_map/all_to_all | solution.py:230

commit v2 on v1

--- a/solution.py
+++ b/solution.py
@@ -19,7 +19,7 @@
     z = jnp.zeros_like(x)
     return jnp.concatenate([jnp.concatenate([x, z], 1), jnp.concatenate([z, y], 1)], 0)
 
-def k1_body(unroll, nbr, ext, sel, corr, mask, d_ref, ot_ref, table, tmp):
+def k1_body(unroll, nbr, ext, sel, corr, mask, d_ref, o_ref, table, tmp):
     step = pl.program_id(0)
     @pl.when(step == 0)
     def _():
@@ -35,22 +35,20 @@
         for r in range(27):
             x = corr[:, pl.ds(pl.multiple_of((c * 27 + r) * 128, 128), 128)].astype(F32)
             tmp[pl.ds(pl.multiple_of((c * 27 + r) * 16, 16), 16), :] = x
-    eye = (lax.broadcasted_iota(jnp.int32, (128, 256), 0) == lax.broadcasted_iota(jnp.int32, (128, 256), 1) % 128).astype(BF)
     pad = jnp.zeros((128 - PR, 128), BF)
     d2 = d_ref.reshape(PR * G, 128)
+    def bdiag(i, h, j):
+        base = (step * G + 2 * i + h) * NK + 8 * j
+        return jnp.concatenate([table[nbr[base + kk]] * mask[kk] for kk in range(8)], 0)
     def pair(i):
-        d = jnp.zeros((PR, 256), F32)
+        o = [[tmp[pl.ds(j * 16 + 2 * i + h, PR, stride=48), :].astype(BF) for j in range(3)] for h in range(2)]
+        ot = [[jnp.concatenate([o[h][j], pad], 0).T for j in range(3)] for h in range(2)]
+        p = []
         for j in range(3):
-            o = [tmp[pl.ds(j * 16 + 2 * i + h, PR, stride=48), :].astype(BF) for h in range(2)]
-            bd = []
-            for h in range(2):
-                base = (step * G + 2 * i + h) * NK + 8 * j
-                bd.append(jnp.concatenate([table[nbr[base + kk]] * mask[kk] for kk in range(8)], 0))
-            p = dot(jnp.concatenate(o, 1), diag(*bd)).astype(BF)
-            rhs = diag(*[jnp.concatenate([v, pad], 0) for v in o])
-            r = dot_nt(jnp.concatenate([p, eye], 0), rhs)
-            d = d + r[:PR]
-            ot_ref[i, j * 128:(j + 1) * 128, :] = r[PR:].astype(BF)
+            both = jnp.concatenate([o[0][j], o[1][j]], 1)
+            o_ref[i, :, j * 256:(j + 1) * 256] = both
+            p.append(dot(both, diag(bdiag(i, 0, j), bdiag(i, 1, j))).astype(BF))
+        d = dot(jnp.concatenate(p, 1), jnp.concatenate([diag(ot[0][j], ot[1][j]) for j in range(3)], 0))
         for h in range(2):
             d2[pl.ds(2 * i + h, PR, stride=G), :] = d[:, h * 128:(h + 1) * 128]
     @pl.loop(0, G // 2 // unroll)
@@ -68,33 +66,40 @@
                       pl.BlockSpec((G, 34560), lambda s, n: (s, 0)),
                       pl.BlockSpec((8, 16, 128), lambda s, n: (0, 0, 0))],
             out_specs=[pl.BlockSpec((PR, G, 128), lambda s, n: (0, s, 0)),
-                       pl.BlockSpec((G // 2, 384, 256), lambda s, n: (s, 0, 0))],
+                       pl.BlockSpec((G // 2, PR, 768), lambda s, n: (s, 0, 0))],
             scratch_shapes=[pltpu.VMEM((9 * A, 16, 128), BF), pltpu.VMEM((288 * 16, 128), F32)]),
-        out_shape=[jax.ShapeDtypeStruct((PR, A, 128), F32), jax.ShapeDtypeStruct((A // 2, 384, 256), BF)],
+        out_shape=[jax.ShapeDtypeStruct((PR, A, 128), F32), jax.ShapeDtypeStruct((A // 2, PR, 768), BF)],
         compiler_params=pltpu.CompilerParams(vmem_limit_bytes=60 << 20, dimension_semantics=("arbitrary",)),
         name="descriptor",
     )(nbr, ext, sel, corr, mask)
 
 def consts():
     i = jnp.arange(256)[:, None]; c = jnp.arange(2048)[None]
-    sel = ((i // 16 == c // 128) & (i % 16 == c % 16)).astype(BF)
+    sel = (((i >> 4) == (c >> 7)) & ((i & 15) == (c & 15))).astype(BF)
     k = jnp.arange(8)[:, None, None]; l = jnp.arange(128)[None, None]
-    mask = jnp.broadcast_to((l // 16 == k), (8, 16, 128)).astype(BF)
+    mask = jnp.broadcast_to(((l >> 4) == k), (8, 16, 128)).astype(BF)
     return sel, mask
 
 def relay(corr):
     return corr.reshape(256, 34560)
 
 PC = 16
-def k2_body(d_ref, w1, b1, w2, b2, w3, b3, ro, e_ref, s_ref, acc, grad):
+def k2_body(d_ref, w1, b1, w2, b2, w3, b3, ro, e_ref, s_ref, acc, grad, rows):
     phase, c = pl.program_id(0), pl.program_id(1)
     last = pl.num_programs(1) - 1
+    pad = jnp.zeros((128 - PR, H), BF)
+    inside = c * (PC * NP) + lax.broadcasted_iota(jnp.int32, (PC * NP, H), 0) < NP * NP
+    rows[:PC * NP, :] = jnp.where(inside, w1[...].astype(F32), 0.0)
+    rows[PC * NP:, :] = jnp.zeros((8, H), F32)
+    def weights(p):
+        w = [rows[NP * v:NP * v + PR, :].astype(BF) for v in (p, p + 1)]
+        return jnp.concatenate([w[0], pad, w[1], pad], 0)
     @pl.when(phase == 0)
     def _():
         t = jnp.zeros((A, H), F32)
         for p in range(0, PC, 2):
             x = jnp.concatenate([d_ref[p], d_ref[p + 1]], 1).astype(BF)
-            t = t + dot(x, w1[p:p + 2].reshape(256, H))
+            t = t + dot(x, weights(p))
         acc[...] = jnp.where(c == 0, 0.0, acc[...]) + t
         @pl.when(c == last)
         def _():
@@ -111,28 +116,28 @@
     @pl.when(phase == 1)
     def _():
         for p in range(0, PC, 2):
-            t = dot_nt(grad[...], w1[p:p + 2].reshape(256, H))
+            t = dot_nt(grad[...], weights(p))
             s_ref[p] = t[:, :128]
             s_ref[p + 1] = t[:, 128:]
 
-def k2(d, w1p, b1, w2, b2, w3, b3, ro):
+def k2(d, w1, b1, w2, b2, w3, b3, ro):
     n = PR // PC
     row = lambda: pl.BlockSpec((1, H), lambda f, c: (0, 0))
     mat = lambda: pl.BlockSpec((H, H), lambda f, c: (0, 0))
     return pl.pallas_call(
         k2_body, grid=(2, n),
         in_specs=[pl.BlockSpec((PC, A, 128), lambda f, c: (jnp.where(f == 0, c, n - 1), 0, 0)),
-                  pl.BlockSpec((PC, 128, H), lambda f, c: (c, 0, 0)),
+                  pl.BlockSpec((PC * NP, H), lambda f, c: (c, 0)),
                   row(), mat(), row(), mat(), row(), row()],
         out_specs=[pl.BlockSpec((A, 1), lambda f, c: (0, 0)),
                    pl.BlockSpec((PC, A, 128), lambda f, c: (jnp.where(f == 0, 0, c), 0, 0))],
-        scratch_shapes=[pltpu.VMEM((A, H), F32), pltpu.VMEM((A, H), BF)],
+        scratch_shapes=[pltpu.VMEM((A, H), F32), pltpu.VMEM((A, H), BF), pltpu.VMEM((PC * NP + 8, H), F32)],
         out_shape=[jax.ShapeDtypeStruct((A, 1), F32), jax.ShapeDtypeStruct((PR, A, 128), F32)],
         compiler_params=pltpu.CompilerParams(vmem_limit_bytes=40 << 20),
         name="network",
-    )(d, w1p, b1, w2, b2, w3, b3, ro)
-
-def k3_body(unroll, nbr, s_ref, ot_ref, fold, out_ref, acc, lift):
+    )(d, w1, b1, w2, b2, w3, b3, ro)
+
+def k3_body(unroll, nbr, s_ref, o_ref, fold, out_ref, acc):
     step = pl.program_id(0)
     @pl.when(step == 0)
     def _():
@@ -143,13 +148,12 @@
     pad = jnp.zeros((128 - PR, 128), BF)
     lane = lax.broadcasted_iota(jnp.int32, (16, 128), 1) // 16
     def pair(i):
-        s = [jnp.concatenate([s2[pl.ds(2 * i + h, PR, stride=G), :].astype(BF), pad], 0) for h in range(2)]
-        lt = dot_nt(ot_ref[i], diag(*s)).astype(BF)
+        st = [jnp.concatenate([s2[pl.ds(2 * i + h, PR, stride=G), :].astype(BF), pad], 0).T for h in range(2)]
+        o = [[jnp.concatenate([o_ref[i, :, j * 256 + h * 128:j * 256 + h * 128 + 128], pad], 0) for j in range(3)] for h in range(2)]
+        ot = jnp.concatenate([jnp.concatenate([o[0][j].T, o[1][j].T], 1) for j in range(3)], 0)
+        lt = dot(ot, diag(*st)).astype(BF)
         for j in range(3):
-            ot = ot_ref[i, j * 128:(j + 1) * 128, :]
-            zero = jnp.zeros((128, 128), BF)
-            rhs = jnp.concatenate([jnp.concatenate([ot[:, :128], zero], 1), jnp.concatenate([zero, ot[:, 128:]], 1)], 0)
-            r = dot_nt(lt[j * 128:(j + 1) * 128], rhs)
+            r = dot(lt[j * 128:(j + 1) * 128], diag(o[0][j], o[1][j]))
             for h in range(2):
                 base = (step * G + 2 * i + h) * NK + 8 * j
                 ns = [nbr[base + kk] for kk in range(8)]
@@ -177,10 +181,10 @@
         grid_spec=pltpu.PrefetchScalarGridSpec(
             num_scalar_prefetch=1, grid=(A // G,),
             in_specs=[pl.BlockSpec((PR, G, 128), lambda s, n: (0, s, 0)),
-                      pl.BlockSpec((G // 2, 384, 256), lambda s, n: (s, 0, 0)),
+                      pl.BlockSpec((G // 2, PR, 768), lambda s, n: (s, 0, 0)),
                       pl.BlockSpec((2048, 256), lambda s, n: (0, 0))],
             out_specs=pl.BlockSpec((9 * A, 256), lambda s, n: (0, 0)),
-            scratch_shapes=[pltpu.VMEM((9 * A, 16, 128), F32), pltpu.VMEM((384, 256), BF)]),
+            scratch_shapes=[pltpu.VMEM((9 * A, 16, 128), F32)]),
         out_shape=jax.ShapeDtypeStruct((9 * A, 256), BF),
         compiler_params=pltpu.CompilerParams(vmem_limit_bytes=60 << 20),
         name="hamilton",
@@ -188,10 +192,7 @@
 
 def fold_of():
     i = jnp.arange(2048)[:, None]; c = jnp.arange(256)[None]
-    return ((i // 128 == c % 16) & (i % 16 == c // 16)).astype(BF)
-
-def w1_of(w):
-    return jnp.pad(w.reshape(NP, NP, H), ((0, PR - NP), (0, 128 - NP), (0, 0)))
+    return (((i >> 7) == (c & 15)) & ((i & 15) == (c >> 4))).astype(BF)
 
 
 def shifted(value, axis, steps):
@@ -211,10 +212,10 @@
     nbr = neighbours.reshape(A * NK)
     ext = padded(density, (("gy", 1), ("gx", 0))).reshape(9 * A, 256)
     row = lambda v: v.reshape(1, H)
-    d, ot = k1(nbr, ext, sel, relay(correlations), mask, 4)
-    energy, slope = k2(d, w1_of(weight_first), row(bias_first), weight_second, row(bias_second),
+    d, ot = k1(nbr, ext, sel, relay(correlations), mask, 8)
+    energy, slope = k2(d, weight_first, row(bias_first), weight_second, row(bias_second),
                        weight_third, row(bias_third), row(readout))
-    part = k3(nbr, slope, ot, fold_of(), 1).reshape(3, 3, A, 256)
+    part = k3(nbr, slope, ot, fold_of(), 8).reshape(3, 3, A, 256)
     folded = part[1].astype(F32)
     for s in (1, -1):
         folded = folded + shifted(part[1 + s], "gx", s).astype(F32)

time: 220 us -> 161 us (0.73)
  Pallas kernels: 142 us -> 94.8 us
  local copies, waits for them, and re-layouts: 19.7 us -> 7.41 us
    pallas_call x1, Pallas kernels: 69.3 us -> 35 us  [k3(): pl.pallas_call(functools.partial(k3_body, unroll), grid_spec=pltpu.Prefet...]
    pallas_call x1, Pallas kernels: 59.4 us -> 44.8 us  [k1(): pl.pallas_call(functools.partial(k1_body, unroll), grid_spec=pltpu.Prefet...]
    reshape x1 -> x0, local copies, waits for them, and re-layouts: 6.89 us -> none  [w1_of(): return jnp.pad(w.reshape(NP, NP, H), ((0, PR - NP), (0, 128 - NP), (0, 0)))]
    pad x1 -> x0, local copies, waits for them, and re-layouts: 5.73 us -> none  [w1_of(): return jnp.pad(w.reshape(NP, NP, H), ((0, PR - NP), (0, 128 - NP), (0, 0)))]
  transfers between devices with their start and end apart: 9 -> 9, of which waited for: 6 -> 7; matrix products, arithmetic and copies ran while one was open for 9% -> 4% of each run, Pallas kernels for 0% -> 0%
where the time goes in v2:
time: 161 us; the launch traced here: 160 us
  Pallas kernels  94.8 us (59%)
  waiting for transfers between devices  25.3 us (16%)
  starting transfers between devices  24.5 us (15%)
  local copies, waits for them, and re-layouts  7.41 us (5%)
  other arithmetic  6.74 us (4%)
    pallas_call x1, Pallas kernels, k1(): pl.pallas_call(functools.partial(k1_body, unroll), grid_spec=pltpu.Prefet...  44.8 us
    pallas_call x1, Pallas kernels, k3(): pl.pallas_call(functools.partial(k3_body, unroll), grid_spec=pltpu.Prefet...  35 us
    pallas_call x1, Pallas kernels, k2(): pl.pallas_call(k2_body, grid=(2, n), in_specs=[pl.BlockSpec((PC, A, 128),...  14.9 us
    ppermute x8, starting transfers between devices, shifted(): lax.ppermute(value, axis, [(s, (s + steps) % count) for s in range(count)])  14.7 us
    ppermute x8, waiting for transfers between devices, shifted(): lax.ppermute(value, axis, [(s, (s + steps) % count) for s in range(count)])  14.5 us
    all_to_all x1, waiting for transfers between devices, on_device(): lax.all_to_all(outgoing, ('gx', 'gy'), split_axis=0, concat_axis=0, tiled...  10.8 us
    all_to_all x1, starting transfers between devices, on_device(): lax.all_to_all(outgoing, ('gx', 'gy'), split_axis=0, concat_axis=0, tiled...  9.75 us
    unnamed x19, local copies, waits for them, and re-layouts  3.96 us
  transfers between devices with their start and end apart: 9, of which 7 were waited for; matrix products, arithmetic and copies ran while one was open for 4% of the time, Pallas kernels for 0%

profile of v2, /device:TPU:1, one launch (start us, length us, event | category | flops | bytes accessed | tf_op | source)
XLA Modules:
  0.0 159.7 jit_solution(12625796757945766554)
XLA Ops:
  0.6 2.1 %collective-permute-start = (bf16[1,1,256,256]{3,2,1,0:T(8,128)(2,1)}, bf16[1,1,256,256]{3,2,1,0:T(8,128)(2,1)S(1)}, u32[]{:S(2)}, u32[]{:S(2)}) collective-permute-start(bf16[1,1,256,256]{3,2,1,0:T(8,128)(2,1)} %param.11), channel_id=1, source_target_pairs={{0,1},{1,2},{2,3},{3,4},{4,5},{5,6},{6,7},{7,8},{8,9},{9,10},{10,1... | collective-permute-start | bytes 393224 | tf_op jit(solution)/shard_map/ppermute | solution.py:200
  2.7 4.8 %collective-permute-start.1 = (bf16[1,1,256,256]{3,2,1,0:T(8,128)(2,1)}, bf16[1,1,256,256]{3,2,1,0:T(8,128)(2,1)S(1)}, u32[]{:S(2)}, u32[]{:S(2)}) collective-permute-start(bf16[1,1,256,256]{3,2,1,0:T(8,128)(2,1)} %param.11), channel_id=1, source_target_pairs={{0,15},{1,0},{2,1},{3,2},{4,3},{5,4},{6,5},{7,6},{8,7},{9,8},{10,9... | collective-permute-start | bytes 393224 | tf_op jit(solution)/shard_map/ppermute | solution.py:200
  7.6 0.8 copy.14
  8.4 0.7 reshape.124.nbr
  9.1 1.3 and_convert_fusion.1.sel
  10.5 0.4 collective-permute-done
  10.9 0.9 constant_dynamic-update-slice_fusion.1
  11.8 0.0 collective-permute-done.1
  11.9 2.4 %collective-permute-start.2 = (bf16[1,3,256,256]{3,2,1,0:T(8,128)(2,1)S(1)}, bf16[1,3,256,256]{3,2,1,0:T(8,128)(2,1)S(1)}, u32[]{:S(2)}, u32[]{:S(2)}) collective-permute-start(bf16[1,3,256,256]{3,2,1,0:T(8,128)(2,1)S(1)} %constant_dynamic-update-slice_fusion), channel_id=1, source_target_pairs={{0,16},{16,32},{32,48},{48,64},{64,80},{80,96},{96,112},{112,0},{1... | collective-permute-start | bytes 1179656 | tf_op jit(solution)/shard_map/ppermute | solution.py:200
  14.3 0.0 collective-permute-start.3
  14.3 2.3 %and_convert_fusion.fold = bf16[2048,256]{1,0:T(8,128)(2,1)} fusion(s32[256]{0:T(256)S(1)} %get-tuple-element.20, s32[256]{0:T(256)S(1)} %get-tuple-element.19, s32[2048]{0:T(1024)S(1)} %get-tuple-element.17, s32[2048]{0:T(1024)S(1)} %get-tuple-element.18), kind=kLoop, calls=%fused_computation | loop fusion | flops 2097152 | bytes 1067008 | tf_op jit(solution)/shard_map/convert_element_type | solution.py:195
  16.6 2.4 %collective-permute-done.2 = bf16[1,3,256,256]{3,2,1,0:T(8,128)(2,1)S(1)} collective-permute-done((bf16[1,3,256,256]{3,2,1,0:T(8,128)(2,1)S(1)}, bf16[1,3,256,256]{3,2,1,0:T(8,128)(2,1)S(1)}, u32[]{:S(2)}, u32[]{:S(2)}) %collective-permute-start.2) | collective-permute-done | bytes 393248 | tf_op jit(solution)/shard_map/ppermute | solution.py:200
  19.0 2.5 %collective-permute-done.3 = bf16[1,3,256,256]{3,2,1,0:T(8,128)(2,1)S(1)} collective-permute-done((bf16[1,3,256,256]{3,2,1,0:T(8,128)(2,1)S(1)}, bf16[1,3,256,256]{3,2,1,0:T(8,128)(2,1)S(1)}, u32[]{:S(2)}, u32[]{:S(2)}) %collective-permute-start.3) | collective-permute-done | bytes 393248 | tf_op jit(solution)/shard_map/ppermute | solution.py:200
  21.5 1.2 pad_maximum_fusion
  22.7 0.6 broadcast_in_dim.2.mask
  23.3 0.0 copy-start.1
  23.3 0.0 copy-start.2
  23.3 0.0 copy-start.5
  23.3 0.0 copy-start.6
  23.3 44.8 %descriptor.1 = (f32[96,256,128]{2,1,0:T(8,128)}, bf16[128,96,768]{2,1,0:T(8,128)(2,1)}) custom-call(s32[6144]{0:T(1024)} %reshape.124.nbr, bf16[2304,256]{1,0:T(8,128)(2,1)} %bitcast.35, bf16[256,2048]{1,0:T(8,128)(2,1)} %and_convert_fusion.1.sel, bf16[256,34560]{1,0:T(8,128)(2,1)} %bitcast.34, bf16[8,16,128]{2,1,0:T(8,128)(2,1)} %broadcast_in_dim.2.mask), custom_call_target="tpu_custom_call" | custom-call | tf_op jit(solution)/shard_map/descriptor/pallas_call | solution.py:60
  68.1 0.0 copy-done.1
  68.1 0.0 copy-done.2
  68.1 0.0 copy-done.3
  68.2 0.0 copy-done.4
  68.2 0.0 copy-done.5
  68.2 0.0 copy-done.6
  68.2 0.0 copy-start
  68.2 2.2 %copy-done = bf16[8100,256]{1,0:T(8,128)(2,1)S(1)} copy-done((bf16[8100,256]{1,0:T(8,128)(2,1)S(1)}, bf16[8100,256]{1,0:T(8,128)(2,1)}, u32[]{:S(2)}) %copy-start) | copy-done | bytes 4147224
  70.4 14.9 %network.1 = (f32[256,1]{1,0:T(8,128)S(1)}, f32[96,256,128]{2,1,0:T(8,128)}) custom-call(f32[96,256,128]{2,1,0:T(8,128)} %get-tuple-element.6.d_ref, bf16[8100,256]{1,0:T(8,128)(2,1)S(1)} %copy-done, f32[1,256]{1,0:T(1,128)S(1)} %bitcast.30, bf16[256,256]{1,0:T(8,128)(2,1)S(1)} %copy-done.1, f32[1,256]{1,0:T(1,128)S(1)} %bitcast.31, ...), custom_call_target="tpu_custom_call" | custom-call | tf_op jit(solution)/shard_map/network/pallas_call | solution.py:127
  85.3 35.0 %hamilton.1 = bf16[2304,256]{1,0:T(8,128)(2,1)} custom-call(s32[6144]{0:T(1024)} %reshape.124.nbr, f32[96,256,128]{2,1,0:T(8,128)} %get-tuple-element.8.s_ref, bf16[128,96,768]{2,1,0:T(8,128)(2,1)} %get-tuple-element.9.o_ref, bf16[2048,256]{1,0:T(8,128)(2,1)} %and_convert_fusion.fold), custom_call_target="tpu_custom_call" | custom-call | tf_op jit(solution)/shard_map/hamilton/pallas_call | solution.py:179
  120.3 1.3 fusion.10
  121.7 0.0 collective-permute-start.4
  121.7 0.5 collective-permute-start.5
  122.2 0.0 copy-done.7
  122.2 0.2 convert_reduce_fusion
  122.4 4.0 %collective-permute-done.4 = bf16[3,256,256]{2,1,0:T(8,128)(2,1)S(1)} collective-permute-done((bf16[3,256,256]{2,1,0:T(8,128)(2,1)S(1)}, bf16[3,256,256]{2,1,0:T(8,128)(2,1)S(1)}, u32[]{:S(2)}, u32[]{:S(2)}) %collective-permute-start.4) | collective-permute-done | bytes 393248 | tf_op jit(solution)/shard_map/ppermute | solution.py:200
  126.4 2.8 %collective-permute-done.5 = bf16[3,256,256]{2,1,0:T(8,128)(2,1)S(1)} collective-permute-done((bf16[3,256,256]{2,1,0:T(8,128)(2,1)S(1)}, bf16[3,256,256]{2,1,0:T(8,128)(2,1)S(1)}, u32[]{:S(2)}, u32[]{:S(2)}) %collective-permute-start.5) | collective-permute-done | bytes 393248 | tf_op jit(solution)/shard_map/ppermute | solution.py:200
  129.2 0.1 fusion.8
  129.4 0.1 collective-permute-start.6
  129.5 4.8 %collective-permute-start.7 = (bf16[256,256]{1,0:T(8,128)(2,1)S(1)}, bf16[256,256]{1,0:T(8,128)(2,1)S(1)}, u32[]{:S(2)}, u32[]{:S(2)}) collective-permute-start(bf16[256,256]{1,0:T(8,128)(2,1)S(1)} %get-tuple-element.16), channel_id=1, source_target_pairs={{0,15},{1,0},{2,1},{3,2},{4,3},{5,4},{6,5},{7,6},{8,7},{9,8},{10,9... | collective-permute-start | bytes 393224 | tf_op jit(solution)/shard_map/ppermute | solution.py:200
  134.2 2.3 %collective-permute-done.6 = bf16[256,256]{1,0:T(8,128)(2,1)S(1)} collective-permute-done((bf16[256,256]{1,0:T(8,128)(2,1)S(1)}, bf16[256,256]{1,0:T(8,128)(2,1)S(1)}, u32[]{:S(2)}, u32[]{:S(2)}) %collective-permute-start.6) | collective-permute-done | bytes 131104 | tf_op jit(solution)/shard_map/ppermute | solution.py:200
  136.6 0.0 collective-permute-done.7
  136.6 0.3 convolution_convert_fusion
  136.8 0.8 reshape.133
  137.6 9.7 %all-to-all-start = ((bf16[128,4,256]{2,1,0:T(4,128)(2,1)}), bf16[128,4,256]{2,1,0:T(4,128)(2,1)S(1)}, u32[]{:S(2)}, u32[]{:S(2)}) async-start(bf16[128,4,256]{2,1,0:T(4,128)(2,1)} %reshape.133), calls=%async_computation | async-start | bytes 524288 | tf_op jit(solution)/shard_map/all_to_all | solution.py:231
  147.4 0.7 reduce
  148.0 10.8 %all-to-all-done = bf16[128,4,256]{2,1,0:T(4,128)(2,1)S(1)} async-done(((bf16[128,4,256]{2,1,0:T(4,128)(2,1)}), bf16[128,4,256]{2,1,0:T(4,128)(2,1)S(1)}, u32[]{:S(2)}, u32[]{:S(2)}) %all-to-all-start) | async-done | bytes 262176 | tf_op jit(solution)/shard_map/all_to_all | solution.py:231
  158.8 0.9 bitcast_convert_fusion
  (11 shorter events, 0.1 us)
Async XLA Ops:
  0.6 10.3 %collective-permute-start = (bf16[1,1,256,256]{3,2,1,0:T(8,128)(2,1)}, bf16[1,1,256,256]{3,2,1,0:T(8,128)(2,1)S(1)}, u32[]{:S(2)}, u32[]{:S(2)}) collective-permute-start(bf16[1,1,256,256]{3,2,1,0:T(8,128)(2,1)} %param.11), channel_id=1, source_target_pairs={{0,1},{1,2},{2,3},{3,4},{4,5},{5,6},{6,7},{7,8},{8,9},{9,10},{10,1... | collective-permute-start | bytes 393224 | tf_op jit(solution)/shard_map/ppermute | solution.py:200
  2.7 9.1 %collective-permute-start.1 = (bf16[1,1,256,256]{3,2,1,0:T(8,128)(2,1)}, bf16[1,1,256,256]{3,2,1,0:T(8,128)(2,1)S(1)}, u32[]{:S(2)}, u32[]{:S(2)}) collective-permute-start(bf16[1,1,256,256]{3,2,1,0:T(8,128)(2,1)} %param.11), channel_id=1, source_target_pairs={{0,15},{1,0},{2,1},{3,2},{4,3},{5,4},{6,5},{7,6},{8,7},{9,8},{10,9... | collective-permute-start | bytes 393224 | tf_op jit(solution)/shard_map/ppermute | solution.py:200
  11.9 7.1 %collective-permute-start.2 = (bf16[1,3,256,256]{3,2,1,0:T(8,128)(2,1)S(1)}, bf16[1,3,256,256]{3,2,1,0:T(8,128)(2,1)S(1)}, u32[]{:S(2)}, u32[]{:S(2)}) collective-permute-start(bf16[1,3,256,256]{3,2,1,0:T(8,128)(2,1)S(1)} %constant_dynamic-update-slice_fusion), channel_id=1, source_target_pairs={{0,16},{16,32},{32,48},{48,64},{64,80},{80,96},{96,112},{112,0},{1... | collective-permute-start | bytes 1179656 | tf_op jit(solution)/shard_map/ppermute | solution.py:200
  14.3 7.2 %collective-permute-start.3 = (bf16[1,3,256,256]{3,2,1,0:T(8,128)(2,1)S(1)}, bf16[1,3,256,256]{3,2,1,0:T(8,128)(2,1)S(1)}, u32[]{:S(2)}, u32[]{:S(2)}) collective-permute-start(bf16[1,3,256,256]{3,2,1,0:T(8,128)(2,1)S(1)} %constant_dynamic-update-slice_fusion), channel_id=1, source_target_pairs={{0,112},{16,0},{32,16},{48,32},{64,48},{80,64},{96,80},{112,96},{1... | collective-permute-start | bytes 1179656 | tf_op jit(solution)/shard_map/ppermute | solution.py:200
  23.3 44.8 %copy-start.1 = (bf16[256,256]{1,0:T(8,128)(2,1)S(1)}, bf16[256,256]{1,0:T(8,128)(2,1)}, u32[]{:S(2)}) copy-start(bf16[256,256]{1,0:T(8,128)(2,1)} %w2.1) | copy-start | bytes 393220
  23.3 44.8 %copy-start.2 = (bf16[256,256]{1,0:T(8,128)(2,1)S(1)}, bf16[256,256]{1,0:T(8,128)(2,1)}, u32[]{:S(2)}) copy-start(bf16[256,256]{1,0:T(8,128)(2,1)} %w3.1) | copy-start | bytes 393220
  23.3 44.8 %copy-start.3 = (f32[256]{0:T(256)S(1)}, f32[256]{0:T(256)}, u32[]{:S(2)}) copy-start(f32[256]{0:T(256)} %param.15) | copy-start | bytes 3076
  23.3 44.9 %copy-start.4 = (f32[256]{0:T(256)S(1)}, f32[256]{0:T(256)}, u32[]{:S(2)}) copy-start(f32[256]{0:T(256)} %param.17) | copy-start | bytes 3076
  23.3 44.9 %copy-start.5 = (f32[256]{0:T(256)S(1)}, f32[256]{0:T(256)}, u32[]{:S(2)}) copy-start(f32[256]{0:T(256)} %param.19) | copy-start | bytes 3076
  23.3 44.9 %copy-start.6 = (f32[256]{0:T(256)S(1)}, f32[256]{0:T(256)}, u32[]{:S(2)}) copy-start(f32[256]{0:T(256)} %param.20) | copy-start | bytes 3076
  68.2 2.2 %copy-start = (bf16[8100,256]{1,0:T(8,128)(2,1)S(1)}, bf16[8100,256]{1,0:T(8,128)(2,1)}, u32[]{:S(2)}) copy-start(bf16[8100,256]{1,0:T(8,128)(2,1)} %w1.1) | copy-start | bytes 12441604
  120.3 1.9 %copy-start.7 = (s32[1,1,256,1]{2,3,1,0:T(1,128)S(1)}, s32[1,1,256,1]{2,3,1,0:T(1,128)}, u32[]{:S(2)}) copy-start(s32[1,1,256,1]{2,3,1,0:T(1,128)} %param.21) | copy-start | bytes 3076
  121.7 4.7 %collective-permute-start.4 = (bf16[3,256,256]{2,1,0:T(8,128)(2,1)S(1)}, bf16[3,256,256]{2,1,0:T(8,128)(2,1)S(1)}, u32[]{:S(2)}, u32[]{:S(2)}) collective-permute-start(bf16[3,256,256]{2,1,0:T(8,128)(2,1)S(1)} %bitcast.38), channel_id=1, source_target_pairs={{0,16},{16,32},{32,48},{48,64},{64,80},{80,96},{96,112},{112,0},{1... | collective-permute-start | bytes 1179656 | tf_op jit(solution)/shard_map/ppermute | solution.py:200
  121.7 7.5 %collective-permute-start.5 = (bf16[3,256,256]{2,1,0:T(8,128)(2,1)S(1)}, bf16[3,256,256]{2,1,0:T(8,128)(2,1)S(1)}, u32[]{:S(2)}, u32[]{:S(2)}) collective-permute-start(bf16[3,256,256]{2,1,0:T(8,128)(2,1)S(1)} %bitcast.37), channel_id=1, source_target_pairs={{0,112},{16,0},{32,16},{48,32},{64,48},{80,64},{96,80},{112,96},{1... | collective-permute-start | bytes 1179656 | tf_op jit(solution)/shard_map/ppermute | solution.py:200
  129.4 7.2 %collective-permute-start.6 = (bf16[256,256]{1,0:T(8,128)(2,1)S(1)}, bf16[256,256]{1,0:T(8,128)(2,1)S(1)}, u32[]{:S(2)}, u32[]{:S(2)}) collective-permute-start(bf16[256,256]{1,0:T(8,128)(2,1)S(1)} %get-tuple-element.15), channel_id=1, source_target_pairs={{0,1},{1,2},{2,3},{3,4},{4,5},{5,6},{6,7},{7,8},{8,9},{9,10},{10,1... | collective-permute-start | bytes 393224 | tf_op jit(solution)/shard_map/ppermute | solution.py:200
  129.5 7.1 %collective-permute-start.7 = (bf16[256,256]{1,0:T(8,128)(2,1)S(1)}, bf16[256,256]{1,0:T(8,128)(2,1)S(1)}, u32[]{:S(2)}, u32[]{:S(2)}) collective-permute-start(bf16[256,256]{1,0:T(8,128)(2,1)S(1)} %get-tuple-element.16), channel_id=1, source_target_pairs={{0,15},{1,0},{2,1},{3,2},{4,3},{5,4},{6,5},{7,6},{8,7},{9,8},{10,9... | collective-permute-start | bytes 393224 | tf_op jit(solution)/shard_map/ppermute | solution.py:200
  137.6 21.2 %all-to-all-start = ((bf16[128,4,256]{2,1,0:T(4,128)(2,1)}), bf16[128,4,256]{2,1,0:T(4,128)(2,1)S(1)}, u32[]{:S(2)}, u32[]{:S(2)}) async-start(bf16[128,4,256]{2,1,0:T(4,128)(2,1)} %reshape.133), calls=%async_computation | async-start | bytes 524288 | tf_op jit(solution)/shard_map/all_to_all | solution.py:231

commit v3 on v2

--- a/solution.py
+++ b/solution.py
@@ -195,41 +195,134 @@
     return (((i >> 7) == (c & 15)) & ((i & 15) == (c >> 4))).astype(BF)
 
 
-def shifted(value, axis, steps):
-    count = lax.axis_size(axis)
-    return lax.ppermute(value, axis, [(s, (s + steps) % count) for s in range(count)])
-
-
-def padded(block, sides):
-    for axis, dim in sides:
-        block = jnp.concatenate([shifted(block, axis, 1), block, shifted(block, axis, -1)], axis=dim)
-    return block
+MESH = pl.DeviceIdType.MESH
+
+
+def greet(peers):
+    barrier = pltpu.get_barrier_semaphore()
+    for peer in peers:
+        pl.semaphore_signal(barrier, inc=1, device_id=peer, device_id_type=MESH)
+    pl.semaphore_wait(barrier, len(peers))
+
+
+def push(src, dst, send, recv, peer):
+    copy = pltpu.make_async_remote_copy(src_ref=src, dst_ref=dst, send_sem=send, recv_sem=recv,
+                                        device_id=peer, device_id_type=MESH)
+    copy.start()
+    return copy
+
+
+def halo_body(nx, ny, own, out, sy, ry, sx, rx):
+    x, y = lax.axis_index("gx"), lax.axis_index("gy")
+    onx = lambda k: {"gx": lax.rem(x + k + nx, nx)}
+    ony = lambda k: {"gy": lax.rem(y + k + ny, ny)}
+    greet([onx(1), onx(-1), ony(1), ony(-1)])
+    out[1, 1] = own[...]
+    first = [push(own, out.at[1, 1 - k], sy.at[(k + 1) // 2], ry.at[(k + 1) // 2], ony(k)) for k in (1, -1)]
+    second = []
+    def spread(j):
+        for k in (1, -1):
+            second.append(push(own if j == 1 else out.at[1, j], out.at[1 - k, j],
+                               sx.at[(k + 1) // 2, j], rx.at[(k + 1) // 2, j], onx(k)))
+    spread(1)
+    for k, copy in zip((1, -1), first):
+        copy.wait_recv()
+        spread(1 - k)
+    for copy in second:
+        copy.wait_recv()
+    for copy in first + second:
+        copy.wait_send()
+
+
+def halo(own, nx, ny):
+    dma = pltpu.SemaphoreType.DMA
+    return pl.pallas_call(
+        functools.partial(halo_body, nx, ny),
+        out_shape=jax.ShapeDtypeStruct((3, 3, A, 256), BF),
+        in_specs=[pl.BlockSpec(memory_space=pltpu.VMEM)],
+        out_specs=pl.BlockSpec(memory_space=pltpu.VMEM),
+        scratch_shapes=[dma((2,)), dma((2,)), dma((2, 3)), dma((2, 3))],
+        compiler_params=pltpu.CompilerParams(collective_id=0, has_side_effects=True),
+        name="halo",
+    )(own)
+
+
+def exchange_body(nx, ny, part, pos, out, near, edge, far, chosen, sent, mid, s1, r1, s2, r2, s3, r3, s4, r4):
+    x, y = lax.axis_index("gx"), lax.axis_index("gy")
+    onx = lambda k: {"gx": lax.rem(x + k + nx, nx)}
+    ony = lambda k: {"gy": lax.rem(y + k + ny, ny)}
+    greet([onx(k) for k in range(1, nx)] + [ony(k) for k in range(1, ny)])
+    first = {}
+    for j in (0, 2, 1):
+        for d, k in enumerate((1, -1)):
+            first[d, j] = push(part.at[1 + k, j], near.at[d, j], s1.at[d, j], r1.at[d, j], onx(k))
+    rows = nx * ny * 8
+    r = lax.broadcasted_iota(jnp.int32, (rows, A), 0)
+    hit = ((r >> 3) * 4 + (r & 3)) == pos[...]
+    half = (r >> 2) & 1
+    for h in range(2):
+        chosen[:, h * A:(h + 1) * A] = jnp.where(hit & (half == h), 1.0, 0.0).astype(BF)
+
+    def fold(j):
+        first[0, j].wait_recv()
+        first[1, j].wait_recv()
+        return part[1, j].astype(F32) + near[0, j].astype(F32) + near[1, j].astype(F32)
+    second = []
+    for d, (j, k) in enumerate(((2, 1), (0, -1))):
+        edge[d] = fold(j).astype(BF)
+        second.append(push(edge.at[d], far.at[d], s2.at[d], r2.at[d], ony(k)))
+    total = fold(1)
+    for d in range(2):
+        second[d].wait_recv()
+        total = total + far[d].astype(F32)
+    both = jnp.concatenate([total[:, :128], total[:, 128:]], 0).astype(BF)
+    sent[...] = dot(chosen[...], both).reshape(nx, ny, 8, 128).astype(BF)
+    third = [push(sent.at[lax.rem(x + k, nx)], mid.at[x], s3.at[k], r3.at[k], onx(k)) for k in range(1, nx)]
+    mid[x] = sent[x]
+    for copy in third:
+        copy.wait_recv()
+    fourth = [push(mid.at[:, lax.rem(y + k, ny)], out.at[:, y], s4.at[k], r4.at[k], ony(k)) for k in range(1, ny)]
+    out[:, y] = mid[:, y]
+    for copy in fourth:
+        copy.wait_recv()
+    for copy in list(first.values()) + second + third + fourth:
+        copy.wait_send()
+
+
+def exchange(part, position, nx, ny):
+    dma = pltpu.SemaphoreType.DMA
+    vmem = pl.BlockSpec(memory_space=pltpu.VMEM)
+    return pl.pallas_call(
+        functools.partial(exchange_body, nx, ny),
+        out_shape=jax.ShapeDtypeStruct((nx, ny, 8, 128), BF),
+        in_specs=[vmem, vmem], out_specs=vmem,
+        scratch_shapes=[pltpu.VMEM((2, 3, A, 256), BF), pltpu.VMEM((2, A, 256), BF), pltpu.VMEM((2, A, 256), BF),
+                        pltpu.VMEM((nx * ny * 8, 2 * A), BF), pltpu.VMEM((nx, ny, 8, 128), BF),
+                        pltpu.VMEM((nx, ny, 8, 128), BF),
+                        dma((2, 3)), dma((2, 3)), dma((2,)), dma((2,)), dma((nx,)), dma((nx,)), dma((ny,)), dma((ny,))],
+        compiler_params=pltpu.CompilerParams(collective_id=1, has_side_effects=True, vmem_limit_bytes=40 << 20),
+        name="exchange",
+    )(part, position)
 
 
 def on_device(density, neighbours, correlations, weight_first, bias_first, weight_second, bias_second,
               weight_third, bias_third, readout, destination):
+    nx, ny = lax.axis_size("gx"), lax.axis_size("gy")
     sel, mask = consts()
     nbr = neighbours.reshape(A * NK)
-    ext = padded(density, (("gy", 1), ("gx", 0))).reshape(9 * A, 256)
+    ext = halo(density.reshape(A, 256), nx, ny).reshape(9 * A, 256)
     row = lambda v: v.reshape(1, H)
-    d, ot = k1(nbr, ext, sel, relay(correlations), mask, 8)
+    d, o = k1(nbr, ext, sel, relay(correlations), mask, 8)
     energy, slope = k2(d, weight_first, row(bias_first), weight_second, row(bias_second),
                        weight_third, row(bias_third), row(readout))
-    part = k3(nbr, slope, ot, fold_of(), 8).reshape(3, 3, A, 256)
-    folded = part[1].astype(F32)
-    for s in (1, -1):
-        folded = folded + shifted(part[1 + s], "gx", s).astype(F32)
-    hamilton = folded[1]
-    for s in (1, -1):
-        hamilton = hamilton + shifted(folded[1 + s].astype(BF), "gy", s).astype(F32)
+    part = k3(nbr, slope, o, fold_of(), 8).reshape(3, 3, A, 256)
     target = destination.reshape(A)
     order = jnp.arange(A, dtype=jnp.int32)
-    earlier = (target[:, None] == target[None, :]) & (order[None, :] < order[:, None])
-    position = target * 4 + jnp.sum(earlier.astype(jnp.int32), axis=1)
-    chosen = (jnp.arange(512, dtype=jnp.int32)[:, None] == position[None, :]).astype(BF)
-    outgoing = dot(chosen, hamilton.astype(BF)).astype(BF).reshape(128, 4, 256)
-    received = lax.all_to_all(outgoing, ("gx", "gy"), split_axis=0, concat_axis=0, tiled=True)
-    return energy.reshape(1, 1, A), received[None].astype(F32)
+    earlier = (target[:, None] == target[None, :]) & (order[:, None] < order[None, :])
+    position = target * 4 + jnp.sum(earlier.astype(jnp.int32), axis=0)
+    received = exchange(part, position.reshape(1, A), nx, ny)
+    blocks = received.reshape(nx * ny, 2, 4, 128).transpose(0, 2, 1, 3).reshape(1, nx * ny, 4, 256).astype(F32)
+    return energy.reshape(1, 1, A), blocks
 
 
 def solution(mesh):

time: 161 us -> 153 us (0.950)
  Pallas kernels: 94.8 us -> 140 us
  waiting for transfers between devices: 25.3 us -> 0 us
  starting transfers between devices: 24.5 us -> 0 us
  local copies, waits for them, and re-layouts: 7.41 us -> 5.63 us
    pallas_call x0 -> x2, Pallas kernels: none -> 45 us  [the longest x1 25 us: exchange(): pl.pallas_call(functools.partial(exchange_body, nx, ny), out_shape=jax.Sh...]
    ppermute x8 -> x0, starting transfers between devices: 14.7 us -> none  [shifted(): lax.ppermute(value, axis, [(s, (s + steps) % count) for s in range(count)])]
    ppermute x8 -> x0, waiting for transfers between devices: 14.5 us -> none  [shifted(): lax.ppermute(value, axis, [(s, (s + steps) % count) for s in range(count)])]
    all_to_all x1 -> x0, waiting for transfers between devices: 10.8 us -> none  [on_device(): lax.all_to_all(outgoing, ('gx', 'gy'), split_axis=0, concat_axis=0, tiled...]
    all_to_all x1 -> x0, starting transfers between devices: 9.75 us -> none  [on_device(): lax.all_to_all(outgoing, ('gx', 'gy'), split_axis=0, concat_axis=0, tiled...]
  transfers between devices with their start and end apart: 9 -> 0, of which waited for: 7 -> 0; matrix products, arithmetic and copies ran while one was open for 4% -> 0% of each run, Pallas kernels for 0% -> 0%
where the time goes in v3:
time: 153 us; the launch traced here: 152 us
  Pallas kernels  140 us (92%)
  local copies, waits for them, and re-layouts  5.63 us (4%)
  other arithmetic  5.39 us (4%)
    pallas_call x1, Pallas kernels, k1(): pl.pallas_call(functools.partial(k1_body, unroll), grid_spec=pltpu.Prefet...  44.9 us
    pallas_call x1, Pallas kernels, k3(): pl.pallas_call(functools.partial(k3_body, unroll), grid_spec=pltpu.Prefet...  35.1 us
    pallas_call x1, Pallas kernels, exchange(): pl.pallas_call(functools.partial(exchange_body, nx, ny), out_shape=jax.Sh...  25 us
    pallas_call x1, Pallas kernels, halo(): pl.pallas_call(functools.partial(halo_body, nx, ny), out_shape=jax.ShapeD...  20 us
    pallas_call x1, Pallas kernels, k2(): pl.pallas_call(k2_body, grid=(2, n), in_specs=[pl.BlockSpec((PC, A, 128),...  14.9 us
    unnamed x19, local copies, waits for them, and re-layouts  4.3 us

profile of v3, /device:TPU:1, one launch (start us, length us, event | category | flops | bytes accessed | tf_op | source)
XLA Modules:
  0.0 151.7 jit_solution(16645970282219591823)
XLA Ops:
  0.7 1.4 and_convert_fusion.1.sel
  2.0 0.8 copy.16
  2.9 0.7 reshape.142.nbr
  3.6 20.0 %halo.1 = bf16[3,3,256,256]{3,2,1,0:T(8,128)(2,1)} custom-call(bf16[256,256]{1,0:T(8,128)(2,1)} %bitcast.31), custom_call_target="tpu_custom_call" | custom-call | tf_op jit(solution)/shard_map/halo/pallas_call | solution.py:239
  23.7 0.6 broadcast_in_dim.2.mask
  24.3 0.0 copy-start.2
  24.3 0.0 copy-start.3
  24.3 0.0 copy-start.4
  24.3 0.0 copy-start.5
  24.3 0.0 copy-start.6
  24.3 0.0 copy-start.7
  24.3 44.9 %descriptor.1 = (f32[96,256,128]{2,1,0:T(8,128)}, bf16[128,96,768]{2,1,0:T(8,128)(2,1)}) custom-call(s32[6144]{0:T(1024)} %reshape.142.nbr, bf16[2304,256]{1,0:T(8,128)(2,1)} %bitcast.29, bf16[256,2048]{1,0:T(8,128)(2,1)} %and_convert_fusion.1.sel, bf16[256,34560]{1,0:T(8,128)(2,1)} %bitcast.28, bf16[8,16,128]{2,1,0:T(8,128)(2,1)} %broadcast_in_dim.2.mask), custom_call_target="tpu_custom_call" | custom-call | tf_op jit(solution)/shard_map/descriptor/pallas_call | solution.py:60
  69.2 0.0 copy-done.2
  69.2 0.0 copy-done.3
  69.2 0.0 copy-done.4
  69.2 0.0 copy-done.5
  69.2 0.0 copy-done.6
  69.3 0.0 copy-done.7
  69.3 0.0 copy-start.1
  69.3 2.2 %copy-done.1 = bf16[8100,256]{1,0:T(8,128)(2,1)S(1)} copy-done((bf16[8100,256]{1,0:T(8,128)(2,1)S(1)}, bf16[8100,256]{1,0:T(8,128)(2,1)}, u32[]{:S(2)}) %copy-start.1) | copy-done | bytes 4147224
  71.4 14.9 %network.1 = (f32[256,1]{1,0:T(8,128)S(1)}, f32[96,256,128]{2,1,0:T(8,128)}) custom-call(f32[96,256,128]{2,1,0:T(8,128)} %get-tuple-element.6.d_ref, bf16[8100,256]{1,0:T(8,128)(2,1)S(1)} %copy-done.1, f32[1,256]{1,0:T(1,128)S(1)} %bitcast.24, bf16[256,256]{1,0:T(8,128)(2,1)S(1)} %copy-done.2, f32[1,256]{1,0:T(1,128)S(1)} %bitcast.25, ...), custom_call_target="tpu_custom_call" | custom-call | tf_op jit(solution)/shard_map/network/pallas_call | solution.py:127
  86.3 2.4 %and_convert_fusion.fold = bf16[2048,256]{1,0:T(8,128)(2,1)} fusion(s32[256]{0:T(256)S(1)} %get-tuple-element.13, s32[256]{0:T(256)S(1)} %get-tuple-element.12, s32[2048]{0:T(1024)S(1)} %get-tuple-element.10, s32[2048]{0:T(1024)S(1)} %get-tuple-element.11), kind=kLoop, calls=%fused_computation | loop fusion | flops 2097152 | bytes 1067008 | tf_op jit(solution)/shard_map/convert_element_type | solution.py:195
  88.7 0.0 copy-start.8
  88.7 35.1 %hamilton.1 = bf16[2304,256]{1,0:T(8,128)(2,1)} custom-call(s32[6144]{0:T(1024)} %reshape.142.nbr, f32[96,256,128]{2,1,0:T(8,128)} %get-tuple-element.8.s_ref, bf16[128,96,768]{2,1,0:T(8,128)(2,1)} %get-tuple-element.9.o_ref, bf16[2048,256]{1,0:T(8,128)(2,1)} %and_convert_fusion.fold), custom_call_target="tpu_custom_call" | custom-call | tf_op jit(solution)/shard_map/hamilton/pallas_call | solution.py:179
  123.8 0.0 copy-done.8
  123.8 0.1 convert_reduce_fusion
  123.9 0.0 copy-start
  123.9 1.3 copy-done
  125.2 25.0 %exchange.1 = bf16[8,16,8,128]{3,2,1,0:T(8,128)(2,1)S(1)} custom-call(bf16[3,3,256,256]{3,2,1,0:T(8,128)(2,1)S(1)} %bitcast.23, s32[1,256]{1,0:T(1,128)S(1)} %bitcast_add_fusion.pos), custom_call_target="tpu_custom_call" | custom-call | tf_op jit(solution)/shard_map/exchange/pallas_call | solution.py:295
  150.2 0.8 convert.6
  151.0 0.7 reduce
  (5 shorter events, 0.0 us)
Async XLA Ops:
  24.3 44.9 %copy-start.2 = (bf16[256,256]{1,0:T(8,128)(2,1)S(1)}, bf16[256,256]{1,0:T(8,128)(2,1)}, u32[]{:S(2)}) copy-start(bf16[256,256]{1,0:T(8,128)(2,1)} %w2.1) | copy-start | bytes 393220
  24.3 44.9 %copy-start.3 = (bf16[256,256]{1,0:T(8,128)(2,1)S(1)}, bf16[256,256]{1,0:T(8,128)(2,1)}, u32[]{:S(2)}) copy-start(bf16[256,256]{1,0:T(8,128)(2,1)} %w3.1) | copy-start | bytes 393220
  24.3 44.9 %copy-start.4 = (f32[256]{0:T(256)S(1)}, f32[256]{0:T(256)}, u32[]{:S(2)}) copy-start(f32[256]{0:T(256)} %param.15) | copy-start | bytes 3076
  24.3 44.9 %copy-start.5 = (f32[256]{0:T(256)S(1)}, f32[256]{0:T(256)}, u32[]{:S(2)}) copy-start(f32[256]{0:T(256)} %param.17) | copy-start | bytes 3076
  24.3 44.9 %copy-start.6 = (f32[256]{0:T(256)S(1)}, f32[256]{0:T(256)}, u32[]{:S(2)}) copy-start(f32[256]{0:T(256)} %param.19) | copy-start | bytes 3076
  24.3 44.9 %copy-start.7 = (f32[256]{0:T(256)S(1)}, f32[256]{0:T(256)}, u32[]{:S(2)}) copy-start(f32[256]{0:T(256)} %param.20) | copy-start | bytes 3076
  69.3 2.2 %copy-start.1 = (bf16[8100,256]{1,0:T(8,128)(2,1)S(1)}, bf16[8100,256]{1,0:T(8,128)(2,1)}, u32[]{:S(2)}) copy-start(bf16[8100,256]{1,0:T(8,128)(2,1)} %w1.1) | copy-start | bytes 12441604
  88.7 35.2 %copy-start.8 = (s32[1,1,256,1]{2,3,1,0:T(1,128)S(1)}, s32[1,1,256,1]{2,3,1,0:T(1,128)}, u32[]{:S(2)}) copy-start(s32[1,1,256,1]{2,3,1,0:T(1,128)} %param.21) | copy-start | bytes 3076
  123.9 1.3 copy-start

commit v4 on v3

--- a/solution.py
+++ b/solution.py
@@ -1,4 +1,5 @@
 import functools
+import numpy as np
 import jax, jax.numpy as jnp
 from jax import lax
 from jax.experimental import pallas as pl
@@ -19,16 +20,21 @@
     z = jnp.zeros_like(x)
     return jnp.concatenate([jnp.concatenate([x, z], 1), jnp.concatenate([z, y], 1)], 0)
 
-def k1_body(unroll, nbr, ext, sel, corr, mask, d_ref, o_ref, table, tmp):
+def k1_body(unroll, nbr, ext, sel, corr, mask, w1_hbm, b1, w2, b2, w3, b3, ro, e_ref, s_hbm, o_ref,
+            table, tmp, d_ref, w1, wide, rows, w_sem, s_sem):
     step = pl.program_id(0)
+    fetch = pltpu.make_async_copy(w1_hbm, w1, w_sem)
     @pl.when(step == 0)
     def _():
+        fetch.start()
         tmp[pl.ds(270 * 16, 18 * 16), :] = jnp.zeros((18 * 16, 128), F32)
         @pl.loop(0, 9)
         def _(b):
-            for o in range(16):
-                t = dot(ext[pl.ds(pl.multiple_of(b * 256, 256), 256), :], sel[:, o * 128:(o + 1) * 128])
-                tmp[pl.ds(o, 256, stride=16), :] = t
+            own = ext[pl.ds(pl.multiple_of(b * 256, 256), 256), :]
+            for o in range(0, 16, 2):
+                t = dot(own, sel[:, o * 128:(o + 2) * 128])
+                for h in range(2):
+                    tmp[pl.ds(o + h, 256, stride=16), :] = t[:, h * 128:(h + 1) * 128]
             table[pl.ds(b * 256, 256)] = tmp[pl.ds(0, 4096), :].reshape(256, 16, 128).astype(BF)
     @pl.loop(0, 10)
     def _(c):
@@ -36,7 +42,7 @@
             x = corr[:, pl.ds(pl.multiple_of((c * 27 + r) * 128, 128), 128)].astype(F32)
             tmp[pl.ds(pl.multiple_of((c * 27 + r) * 16, 16), 16), :] = x
     pad = jnp.zeros((128 - PR, 128), BF)
-    d2 = d_ref.reshape(PR * G, 128)
+    d2 = d_ref.reshape(PR * A, 128)
     def bdiag(i, h, j):
         base = (step * G + 2 * i + h) * NK + 8 * j
         return jnp.concatenate([table[nbr[base + kk]] * mask[kk] for kk in range(8)], 0)
@@ -50,13 +56,53 @@
             p.append(dot(both, diag(bdiag(i, 0, j), bdiag(i, 1, j))).astype(BF))
         d = dot(jnp.concatenate(p, 1), jnp.concatenate([diag(ot[0][j], ot[1][j]) for j in range(3)], 0))
         for h in range(2):
-            d2[pl.ds(2 * i + h, PR, stride=G), :] = d[:, h * 128:(h + 1) * 128]
+            d2[pl.ds(step * G + 2 * i + h, PR, stride=A), :] = d[:, h * 128:(h + 1) * 128]
     @pl.loop(0, G // 2 // unroll)
     def _(i):
         for u in range(unroll):
             pair(i * unroll + u)
-
-def k1(nbr, ext, sel, corr, mask, unroll=1):
+    @pl.when(step == pl.num_programs(0) - 1)
+    def _():
+        fetch.wait()
+        gap = jnp.zeros((128 - PR, H), BF)
+        t = jnp.zeros((A, H), F32)
+        for c in range(PR // PC):
+            n = min(PC * NP, NP * NP - c * PC * NP)
+            rows[:n, :] = w1[c * PC * NP:c * PC * NP + n, :].astype(F32)
+            rows[n:n + 8, :] = jnp.zeros((8, H), F32)
+            for v in range(0, n // NP, 2):
+                w = [rows[NP * u:NP * u + PR, :].astype(BF) for u in (v, v + 1)]
+                w = jnp.concatenate([w[0], gap, w[1], gap], 0)
+                p = c * PC + v
+                wide[p // 2] = w
+                t = t + dot(jnp.concatenate([d_ref[p], d_ref[p + 1]], 1).astype(BF), w)
+        act1 = jnp.tanh(t + b1[...])
+        th2 = jnp.tanh(dot(act1.astype(BF), w2[...]) + b2[...])
+        act2 = act1 + th2
+        th3 = jnp.tanh(dot(act2.astype(BF), w3[...]) + b3[...])
+        e_ref[...] = jnp.sum(((act2 + th3) * ro[...]).T, axis=0, keepdims=True)
+        g3 = (ro[...] * (1.0 - th3 * th3)).astype(BF)
+        back2 = ro[...] + dot_nt(g3, w3[...])
+        g2 = (back2 * (1.0 - th2 * th2)).astype(BF)
+        back1 = back2 + dot_nt(g2, w2[...])
+        g1 = (back1 * (1.0 - act1 * act1)).astype(BF)
+        out = []
+        for c in range(PR // PC):
+            for p in range(c * PC, (c + 1) * PC, 2):
+                if p < NP:
+                    r = dot_nt(g1, wide[p // 2])
+                    d_ref[p] = r[:, :128]
+                    d_ref[p + 1] = r[:, 128:]
+            here = pl.ds(c * PC, PC)
+            out.append(pltpu.make_async_copy(d_ref.at[here], s_hbm.at[here], s_sem.at[c]))
+            out[-1].start()
+        for copy in out:
+            copy.wait()
+
+PC = 16
+def k1(nbr, ext, sel, corr, mask, w1, b1, w2, b2, w3, b3, ro, unroll=8):
+    row = lambda: pl.BlockSpec((1, H), lambda s, n: (0, 0))
+    mat = lambda: pl.BlockSpec((H, H), lambda s, n: (0, 0))
     return pl.pallas_call(
         functools.partial(k1_body, unroll),
         grid_spec=pltpu.PrefetchScalarGridSpec(
@@ -64,78 +110,31 @@
             in_specs=[pl.BlockSpec((9 * A, 256), lambda s, n: (0, 0)),
                       pl.BlockSpec((256, 2048), lambda s, n: (0, 0)),
                       pl.BlockSpec((G, 34560), lambda s, n: (s, 0)),
-                      pl.BlockSpec((8, 16, 128), lambda s, n: (0, 0, 0))],
-            out_specs=[pl.BlockSpec((PR, G, 128), lambda s, n: (0, s, 0)),
+                      pl.BlockSpec((8, 16, 128), lambda s, n: (0, 0, 0)),
+                      pl.BlockSpec(memory_space=pl.ANY),
+                      row(), mat(), row(), mat(), row(), row()],
+            out_specs=[pl.BlockSpec((1, A), lambda s, n: (0, 0)),
+                       pl.BlockSpec(memory_space=pl.ANY),
                        pl.BlockSpec((G // 2, PR, 768), lambda s, n: (s, 0, 0))],
-            scratch_shapes=[pltpu.VMEM((9 * A, 16, 128), BF), pltpu.VMEM((288 * 16, 128), F32)]),
-        out_shape=[jax.ShapeDtypeStruct((PR, A, 128), F32), jax.ShapeDtypeStruct((A // 2, PR, 768), BF)],
+            scratch_shapes=[pltpu.VMEM((9 * A, 16, 128), BF), pltpu.VMEM((288 * 16, 128), F32),
+                            pltpu.VMEM((PR, A, 128), F32), pltpu.VMEM((NP * NP, H), BF),
+                            pltpu.VMEM((NP // 2, 256, H), BF), pltpu.VMEM((PC * NP + 8, H), F32),
+                            pltpu.SemaphoreType.DMA, pltpu.SemaphoreType.DMA((PR // PC,))]),
+        out_shape=[jax.ShapeDtypeStruct((1, A), F32), jax.ShapeDtypeStruct((PR, A, 128), F32),
+                   jax.ShapeDtypeStruct((A // 2, PR, 768), BF)],
         compiler_params=pltpu.CompilerParams(vmem_limit_bytes=60 << 20, dimension_semantics=("arbitrary",)),
         name="descriptor",
-    )(nbr, ext, sel, corr, mask)
+    )(nbr, ext, sel, corr, mask, w1, b1, w2, b2, w3, b3, ro)
 
 def consts():
-    i = jnp.arange(256)[:, None]; c = jnp.arange(2048)[None]
+    i = np.arange(256)[:, None]; c = np.arange(2048)[None]
     sel = (((i >> 4) == (c >> 7)) & ((i & 15) == (c & 15))).astype(BF)
     k = jnp.arange(8)[:, None, None]; l = jnp.arange(128)[None, None]
     mask = jnp.broadcast_to(((l >> 4) == k), (8, 16, 128)).astype(BF)
-    return sel, mask
+    return jnp.asarray(sel), jnp.asarray(mask)
 
 def relay(corr):
     return corr.reshape(256, 34560)
-
-PC = 16
-def k2_body(d_ref, w1, b1, w2, b2, w3, b3, ro, e_ref, s_ref, acc, grad, rows):
-    phase, c = pl.program_id(0), pl.program_id(1)
-    last = pl.num_programs(1) - 1
-    pad = jnp.zeros((128 - PR, H), BF)
-    inside = c * (PC * NP) + lax.broadcasted_iota(jnp.int32, (PC * NP, H), 0) < NP * NP
-    rows[:PC * NP, :] = jnp.where(inside, w1[...].astype(F32), 0.0)
-    rows[PC * NP:, :] = jnp.zeros((8, H), F32)
-    def weights(p):
-        w = [rows[NP * v:NP * v + PR, :].astype(BF) for v in (p, p + 1)]
-        return jnp.concatenate([w[0], pad, w[1], pad], 0)
-    @pl.when(phase == 0)
-    def _():
-        t = jnp.zeros((A, H), F32)
-        for p in range(0, PC, 2):
-            x = jnp.concatenate([d_ref[p], d_ref[p + 1]], 1).astype(BF)
-            t = t + dot(x, weights(p))
-        acc[...] = jnp.where(c == 0, 0.0, acc[...]) + t
-        @pl.when(c == last)
-        def _():
-            act1 = jnp.tanh(acc[...] + b1[...])
-            th2 = jnp.tanh(dot(act1.astype(BF), w2[...]) + b2[...])
-            act2 = act1 + th2
-            th3 = jnp.tanh(dot(act2.astype(BF), w3[...]) + b3[...])
-            e_ref[...] = jnp.sum((act2 + th3) * ro[...], axis=1, keepdims=True)
-            g3 = (ro[...] * (1.0 - th3 * th3)).astype(BF)
-            back2 = ro[...] + dot_nt(g3, w3[...])
-            g2 = (back2 * (1.0 - th2 * th2)).astype(BF)
-            back1 = back2 + dot_nt(g2, w2[...])
-            grad[...] = (back1 * (1.0 - act1 * act1)).astype(BF)
-    @pl.when(phase == 1)
-    def _():
-        for p in range(0, PC, 2):
-            t = dot_nt(grad[...], weights(p))
-            s_ref[p] = t[:, :128]
-            s_ref[p + 1] = t[:, 128:]
-
-def k2(d, w1, b1, w2, b2, w3, b3, ro):
-    n = PR // PC
-    row = lambda: pl.BlockSpec((1, H), lambda f, c: (0, 0))
-    mat = lambda: pl.BlockSpec((H, H), lambda f, c: (0, 0))
-    return pl.pallas_call(
-        k2_body, grid=(2, n),
-        in_specs=[pl.BlockSpec((PC, A, 128), lambda f, c: (jnp.where(f == 0, c, n - 1), 0, 0)),
-                  pl.BlockSpec((PC * NP, H), lambda f, c: (c, 0)),
-                  row(), mat(), row(), mat(), row(), row()],
-        out_specs=[pl.BlockSpec((A, 1), lambda f, c: (0, 0)),
-                   pl.BlockSpec((PC, A, 128), lambda f, c: (jnp.where(f == 0, 0, c), 0, 0))],
-        scratch_shapes=[pltpu.VMEM((A, H), F32), pltpu.VMEM((A, H), BF), pltpu.VMEM((PC * NP + 8, H), F32)],
-        out_shape=[jax.ShapeDtypeStruct((A, 1), F32), jax.ShapeDtypeStruct((PR, A, 128), F32)],
-        compiler_params=pltpu.CompilerParams(vmem_limit_bytes=40 << 20),
-        name="network",
-    )(d, w1, b1, w2, b2, w3, b3, ro)
 
 def k3_body(unroll, nbr, s_ref, o_ref, fold, out_ref, acc):
     step = pl.program_id(0)
@@ -169,10 +168,7 @@
         acc2 = acc.reshape(9 * A * 16, 128)
         @pl.loop(0, 9)
         def _(b):
-            t = jnp.zeros((256, 256), F32)
-            for q in range(0, 16, 2):
-                x = jnp.concatenate([acc2[pl.ds(b * 4096 + q + h, 256, stride=16), :] for h in range(2)], 1).astype(BF)
-                t = t + dot(x, fold[q * 128:(q + 2) * 128, :])
+            t = dot(jnp.concatenate([acc2[pl.ds(b * 4096 + q, 256, stride=16), :].astype(BF) for q in range(16)], 1), fold[...])
             out_ref[pl.ds(pl.multiple_of(b * 256, 256), 256), :] = t.astype(BF)
 
 def k3(nbr, s, ot, fold, unroll=1):
@@ -191,8 +187,8 @@
     )(nbr, s, ot, fold)
 
 def fold_of():
-    i = jnp.arange(2048)[:, None]; c = jnp.arange(256)[None]
-    return (((i >> 7) == (c & 15)) & ((i & 15) == (c >> 4))).astype(BF)
+    i = np.arange(2048)[:, None]; c = np.arange(256)[None]
+    return jnp.asarray((((i >> 7) == (c & 15)) & ((i & 15) == (c >> 4))).astype(BF))
 
 
 MESH = pl.DeviceIdType.MESH
@@ -247,10 +243,12 @@
     )(own)
 
 
-def exchange_body(nx, ny, part, pos, out, near, edge, far, chosen, sent, mid, s1, r1, s2, r2, s3, r3, s4, r4):
+def exchange_body(nx, ny, part, pos, out, mine, near, edge, far, chosen, sent, mid, sm, s1, r1, s2, r2, s3, r3, s4, r4):
     x, y = lax.axis_index("gx"), lax.axis_index("gy")
     onx = lambda k: {"gx": lax.rem(x + k + nx, nx)}
     ony = lambda k: {"gy": lax.rem(y + k + ny, ny)}
+    take = pltpu.make_async_copy(part.at[1], mine, sm)
+    take.start()
     greet([onx(k) for k in range(1, nx)] + [ony(k) for k in range(1, ny)])
     first = {}
     for j in (0, 2, 1):
@@ -263,10 +261,12 @@
     for h in range(2):
         chosen[:, h * A:(h + 1) * A] = jnp.where(hit & (half == h), 1.0, 0.0).astype(BF)
 
+    take.wait()
+
     def fold(j):
         first[0, j].wait_recv()
         first[1, j].wait_recv()
-        return part[1, j].astype(F32) + near[0, j].astype(F32) + near[1, j].astype(F32)
+        return mine[j].astype(F32) + near[0, j].astype(F32) + near[1, j].astype(F32)
     second = []
     for d, (j, k) in enumerate(((2, 1), (0, -1))):
         edge[d] = fold(j).astype(BF)
@@ -295,11 +295,11 @@
     return pl.pallas_call(
         functools.partial(exchange_body, nx, ny),
         out_shape=jax.ShapeDtypeStruct((nx, ny, 8, 128), BF),
-        in_specs=[vmem, vmem], out_specs=vmem,
-        scratch_shapes=[pltpu.VMEM((2, 3, A, 256), BF), pltpu.VMEM((2, A, 256), BF), pltpu.VMEM((2, A, 256), BF),
+        in_specs=[pl.BlockSpec(memory_space=pl.ANY), vmem], out_specs=vmem,
+        scratch_shapes=[pltpu.VMEM((3, A, 256), BF), pltpu.VMEM((2, 3, A, 256), BF), pltpu.VMEM((2, A, 256), BF), pltpu.VMEM((2, A, 256), BF),
                         pltpu.VMEM((nx * ny * 8, 2 * A), BF), pltpu.VMEM((nx, ny, 8, 128), BF),
                         pltpu.VMEM((nx, ny, 8, 128), BF),
-                        dma((2, 3)), dma((2, 3)), dma((2,)), dma((2,)), dma((nx,)), dma((nx,)), dma((ny,)), dma((ny,))],
+                        dma, dma((2, 3)), dma((2, 3)), dma((2,)), dma((2,)), dma((nx,)), dma((nx,)), dma((ny,)), dma((ny,))],
         compiler_params=pltpu.CompilerParams(collective_id=1, has_side_effects=True, vmem_limit_bytes=40 << 20),
         name="exchange",
     )(part, position)
@@ -312,9 +312,8 @@
     nbr = neighbours.reshape(A * NK)
     ext = halo(density.reshape(A, 256), nx, ny).reshape(9 * A, 256)
     row = lambda v: v.reshape(1, H)
-    d, o = k1(nbr, ext, sel, relay(correlations), mask, 8)
-    energy, slope = k2(d, weight_first, row(bias_first), weight_second, row(bias_second),
-                       weight_third, row(bias_third), row(readout))
+    energy, slope, o = k1(nbr, ext, sel, relay(correlations), mask, weight_first, row(bias_first), weight_second,
+                          row(bias_second), weight_third, row(bias_third), row(readout))
     part = k3(nbr, slope, o, fold_of(), 8).reshape(3, 3, A, 256)
     target = destination.reshape(A)
     order = jnp.arange(A, dtype=jnp.int32)

time: 153 us -> 141 us (0.922)
  Pallas kernels: 140 us -> 135 us
  other arithmetic: 5.39 us -> 0.96 us
  local copies, waits for them, and re-layouts: 5.63 us -> 3.45 us
    pallas_call x1 -> x0, Pallas kernels: 14.9 us -> none  [k2(): pl.pallas_call(k2_body, grid=(2, n), in_specs=[pl.BlockSpec((PC, A, 128),...]
    pallas_call x1, Pallas kernels: 44.9 us -> 54.4 us  [k1(): pl.pallas_call(functools.partial(k1_body, unroll), grid_spec=pltpu.Prefet...]
    convert_element_type x2 -> x0, other arithmetic: 3.75 us -> none  [the longest x1 2.35 us: fold_of(): return ((i >> 7 == c & 15) & (i & 15 == c >> 4)).astype(BF)]
    unnamed x19 -> x5, local copies, waits for them, and re-layouts: 4.3 us -> 2.11 us
where the time goes in v4:
time: 141 us; the launch traced here: 140 us
  Pallas kernels  135 us (96%)
  local copies, waits for them, and re-layouts  3.45 us (2%)
    pallas_call x1, Pallas kernels, k1(): pl.pallas_call(functools.partial(k1_body, unroll), grid_spec=pltpu.Prefet...  54.4 us
    pallas_call x1, Pallas kernels, k3(): pl.pallas_call(functools.partial(k3_body, unroll), grid_spec=pltpu.Prefet...  35.1 us
    pallas_call x1, Pallas kernels, exchange(): pl.pallas_call(functools.partial(exchange_body, nx, ny), out_shape=jax.Sh...  25.3 us
    pallas_call x1, Pallas kernels, halo(): pl.pallas_call(functools.partial(halo_body, nx, ny), out_shape=jax.ShapeD...  20.1 us

profile of v4, /device:TPU:1, one launch (start us, length us, event | category | flops | bytes accessed | tf_op | source)
XLA Modules:
  0.0 140.0 jit_solution(8967594483110332744)
XLA Ops:
  0.6 0.8 copy.18
  1.5 0.7 reshape.102.nbr
  2.2 20.1 %halo.1 = bf16[3,3,256,256]{3,2,1,0:T(8,128)(2,1)} custom-call(bf16[256,256]{1,0:T(8,128)(2,1)} %bitcast.27), custom_call_target="tpu_custom_call" | custom-call | tf_op jit(solution)/shard_map/halo/pallas_call | solution.py:235
  22.3 0.6 broadcast_in_dim.2.mask
  22.9 54.4 %descriptor.1 = (f32[1,256]{1,0:T(1,128)}, f32[96,256,128]{2,1,0:T(8,128)}, bf16[128,96,768]{2,1,0:T(8,128)(2,1)}) custom-call(s32[6144]{0:T(1024)} %reshape.102.nbr, bf16[2304,256]{1,0:T(8,128)(2,1)} %bitcast.25, bf16[256,2048]{1,0:T(8,128)(2,1)} %constant.3.clone.sel, bf16[256,34560]{1,0:T(8,128)(2,1)} %bitcast.24, ...), custom_call_target="tpu_custom_call" | custom-call | tf_op jit(solution)/shard_map/descriptor/pallas_call | solution.py:106
  77.3 0.0 copy-start.1
  77.3 35.1 %hamilton.1 = bf16[2304,256]{1,0:T(8,128)(2,1)} custom-call(s32[6144]{0:T(1024)} %reshape.102.nbr, f32[96,256,128]{2,1,0:T(8,128)} %get-tuple-element.6.s_ref, bf16[128,96,768]{2,1,0:T(8,128)(2,1)} %get-tuple-element.7.o_ref, bf16[2048,256]{1,0:T(8,128)(2,1)} %constant.10.clone.fold), custom_call_target="tpu_custom_call" | custom-call | tf_op jit(solution)/shard_map/hamilton/pallas_call | solution.py:175
  112.5 0.0 copy-done.1
  112.5 0.1 convert_reduce_fusion
  112.6 0.0 copy-start
  112.6 1.3 copy-done
  113.9 25.3 %exchange.1 = bf16[8,16,8,128]{3,2,1,0:T(8,128)(2,1)S(1)} custom-call(bf16[3,3,256,256]{3,2,1,0:T(8,128)(2,1)S(1)} %bitcast.23, s32[1,256]{1,0:T(1,128)S(1)} %bitcast_add_fusion.pos), custom_call_target="tpu_custom_call" | custom-call | tf_op jit(solution)/shard_map/exchange/pallas_call | solution.py:295
  139.1 0.8 convert.6
  (3 shorter events, 0.0 us)
Async XLA Ops:
  77.3 35.2 %copy-start.1 = (s32[1,1,256,1]{2,3,1,0:T(1,128)S(1)}, s32[1,1,256,1]{2,3,1,0:T(1,128)}, u32[]{:S(2)}) copy-start(s32[1,1,256,1]{2,3,1,0:T(1,128)} %param.23) | copy-start | bytes 3076
  112.6 1.3 copy-start

commit v5 on v4

--- a/solution.py
+++ b/solution.py
@@ -20,14 +20,16 @@
     z = jnp.zeros_like(x)
     return jnp.concatenate([jnp.concatenate([x, z], 1), jnp.concatenate([z, y], 1)], 0)
 
-def k1_body(unroll, nbr, ext, sel, corr, mask, w1_hbm, b1, w2, b2, w3, b3, ro, e_ref, s_hbm, o_ref,
-            table, tmp, d_ref, w1, wide, rows, w_sem, s_sem):
+def k1_body(unroll, nbr, ext, sel, o_ref, w1_hbm, b1, w2, b2, w3, b3, ro, e_ref, s_hbm,
+            table, tmp, mask, d_ref, w1, wide, rows, w_sem, s_sem):
     step = pl.program_id(0)
     fetch = pltpu.make_async_copy(w1_hbm, w1, w_sem)
     @pl.when(step == 0)
     def _():
         fetch.start()
-        tmp[pl.ds(270 * 16, 18 * 16), :] = jnp.zeros((18 * 16, 128), F32)
+        lane = lax.broadcasted_iota(jnp.int32, (16, 128), 1) >> 4
+        for kk in range(8):
+            mask[kk] = jnp.where(lane == kk, 1.0, 0.0).astype(BF)
         @pl.loop(0, 9)
         def _(b):
             own = ext[pl.ds(pl.multiple_of(b * 256, 256), 256), :]
@@ -36,24 +38,16 @@
                 for h in range(2):
                     tmp[pl.ds(o + h, 256, stride=16), :] = t[:, h * 128:(h + 1) * 128]
             table[pl.ds(b * 256, 256)] = tmp[pl.ds(0, 4096), :].reshape(256, 16, 128).astype(BF)
-    @pl.loop(0, 10)
-    def _(c):
-        for r in range(27):
-            x = corr[:, pl.ds(pl.multiple_of((c * 27 + r) * 128, 128), 128)].astype(F32)
-            tmp[pl.ds(pl.multiple_of((c * 27 + r) * 16, 16), 16), :] = x
     pad = jnp.zeros((128 - PR, 128), BF)
     d2 = d_ref.reshape(PR * A, 128)
     def bdiag(i, h, j):
-        base = (step * G + 2 * i + h) * NK + 8 * j
-        return jnp.concatenate([table[nbr[base + kk]] * mask[kk] for kk in range(8)], 0)
+        return jnp.concatenate([table[nbr[step * G + 2 * i + h, 8 * j + kk]] * mask[kk] for kk in range(8)], 0)
     def pair(i):
-        o = [[tmp[pl.ds(j * 16 + 2 * i + h, PR, stride=48), :].astype(BF) for j in range(3)] for h in range(2)]
+        o = [[o_ref[i, :, j * 256 + h * 128:j * 256 + h * 128 + 128] for j in range(3)] for h in range(2)]
         ot = [[jnp.concatenate([o[h][j], pad], 0).T for j in range(3)] for h in range(2)]
         p = []
         for j in range(3):
-            both = jnp.concatenate([o[0][j], o[1][j]], 1)
-            o_ref[i, :, j * 256:(j + 1) * 256] = both
-            p.append(dot(both, diag(bdiag(i, 0, j), bdiag(i, 1, j))).astype(BF))
+            p.append(dot(o_ref[i, :, j * 256:(j + 1) * 256], diag(bdiag(i, 0, j), bdiag(i, 1, j))).astype(BF))
         d = dot(jnp.concatenate(p, 1), jnp.concatenate([diag(ot[0][j], ot[1][j]) for j in range(3)], 0))
         for h in range(2):
             d2[pl.ds(step * G + 2 * i + h, PR, stride=A), :] = d[:, h * 128:(h + 1) * 128]
@@ -100,7 +94,7 @@
             copy.wait()
 
 PC = 16
-def k1(nbr, ext, sel, corr, mask, w1, b1, w2, b2, w3, b3, ro, unroll=8):
+def k1(nbr, ext, sel, o, w1, b1, w2, b2, w3, b3, ro, unroll=8):
     row = lambda: pl.BlockSpec((1, H), lambda s, n: (0, 0))
     mat = lambda: pl.BlockSpec((H, H), lambda s, n: (0, 0))
     return pl.pallas_call(
@@ -109,29 +103,24 @@
             num_scalar_prefetch=1, grid=(A // G,),
             in_specs=[pl.BlockSpec((9 * A, 256), lambda s, n: (0, 0)),
                       pl.BlockSpec((256, 2048), lambda s, n: (0, 0)),
-                      pl.BlockSpec((G, 34560), lambda s, n: (s, 0)),
-                      pl.BlockSpec((8, 16, 128), lambda s, n: (0, 0, 0)),
+                      pl.BlockSpec((G // 2, PR, 768), lambda s, n: (s, 0, 0)),
                       pl.BlockSpec(memory_space=pl.ANY),
                       row(), mat(), row(), mat(), row(), row()],
             out_specs=[pl.BlockSpec((1, A), lambda s, n: (0, 0)),
-                       pl.BlockSpec(memory_space=pl.ANY),
-                       pl.BlockSpec((G // 2, PR, 768), lambda s, n: (s, 0, 0))],
-            scratch_shapes=[pltpu.VMEM((9 * A, 16, 128), BF), pltpu.VMEM((288 * 16, 128), F32),
+                       pl.BlockSpec(memory_space=pl.ANY)],
+            scratch_shapes=[pltpu.VMEM((9 * A, 16, 128), BF), pltpu.VMEM((4096, 128), F32), pltpu.VMEM((8, 16, 128), BF),
                             pltpu.VMEM((PR, A, 128), F32), pltpu.VMEM((NP * NP, H), BF),
                             pltpu.VMEM((NP // 2, 256, H), BF), pltpu.VMEM((PC * NP + 8, H), F32),
                             pltpu.SemaphoreType.DMA, pltpu.SemaphoreType.DMA((PR // PC,))]),
-        out_shape=[jax.ShapeDtypeStruct((1, A), F32), jax.ShapeDtypeStruct((PR, A, 128), F32),
-                   jax.ShapeDtypeStruct((A // 2, PR, 768), BF)],
+        out_shape=[jax.ShapeDtypeStruct((1, A), F32), jax.ShapeDtypeStruct((PR, A, 128), F32)],
         compiler_params=pltpu.CompilerParams(vmem_limit_bytes=60 << 20, dimension_semantics=("arbitrary",)),
         name="descriptor",
-    )(nbr, ext, sel, corr, mask, w1, b1, w2, b2, w3, b3, ro)
+    )(nbr, ext, sel, o, w1, b1, w2, b2, w3, b3, ro)
 
 def consts():
     i = np.arange(256)[:, None]; c = np.arange(2048)[None]
     sel = (((i >> 4) == (c >> 7)) & ((i & 15) == (c & 15))).astype(BF)
-    k = jnp.arange(8)[:, None, None]; l = jnp.arange(128)[None, None]
-    mask = jnp.broadcast_to(((l >> 4) == k), (8, 16, 128)).astype(BF)
-    return jnp.asarray(sel), jnp.asarray(mask)
+    return jnp.asarray(sel)
 
 def relay(corr):
     return corr.reshape(256, 34560)
@@ -154,8 +143,7 @@
         for j in range(3):
             r = dot(lt[j * 128:(j + 1) * 128], diag(o[0][j], o[1][j]))
             for h in range(2):
-                base = (step * G + 2 * i + h) * NK + 8 * j
-                ns = [nbr[base + kk] for kk in range(8)]
+                ns = [nbr[step * G + 2 * i + h, 8 * j + kk] for kk in range(8)]
                 new = [acc[ns[kk]] + r[kk * 16:(kk + 1) * 16, h * 128:(h + 1) * 128] for kk in range(8)]
                 for kk in range(8):
                     pltpu.store(acc.at[ns[kk]], new[kk], mask=lane == kk)
@@ -208,39 +196,65 @@
     return copy
 
 
-def halo_body(nx, ny, own, out, sy, ry, sx, rx):
+def halo_body(nx, ny, own, corr, out, o_ref, tmp, keep, sy, ry, sx, rx):
+    step = pl.program_id(0)
     x, y = lax.axis_index("gx"), lax.axis_index("gy")
     onx = lambda k: {"gx": lax.rem(x + k + nx, nx)}
     ony = lambda k: {"gy": lax.rem(y + k + ny, ny)}
-    greet([onx(1), onx(-1), ony(1), ony(-1)])
-    out[1, 1] = own[...]
-    first = [push(own, out.at[1, 1 - k], sy.at[(k + 1) // 2], ry.at[(k + 1) // 2], ony(k)) for k in (1, -1)]
-    second = []
-    def spread(j):
-        for k in (1, -1):
-            second.append(push(own if j == 1 else out.at[1, j], out.at[1 - k, j],
-                               sx.at[(k + 1) // 2, j], rx.at[(k + 1) // 2, j], onx(k)))
-    spread(1)
-    for k, copy in zip((1, -1), first):
-        copy.wait_recv()
-        spread(1 - k)
-    for copy in second:
-        copy.wait_recv()
-    for copy in first + second:
-        copy.wait_send()
-
-
-def halo(own, nx, ny):
+    local = pltpu.make_async_copy(own, out.at[1, 1], keep)
+    sends = lambda src, dst, *where: pltpu.make_async_remote_copy(
+        src_ref=src, dst_ref=dst, send_sem=where[0], recv_sem=where[1], device_id=where[2], device_id_type=MESH)
+    first = [sends(own, out.at[1, 1 - k], sy.at[(k + 1) // 2], ry.at[(k + 1) // 2], ony(k)) for k in (1, -1)]
+    spread = [[sends(own if j == 1 else out.at[1, j], out.at[1 - k, j], sx.at[(k + 1) // 2, j], rx.at[(k + 1) // 2, j], onx(k))
+               for k in (1, -1)] for j in range(3)]
+    @pl.when(step == 0)
+    def _():
+        tmp[pl.ds(270 * 16, 18 * 16), :] = jnp.zeros((18 * 16, 128), F32)
+        local.start()
+        greet([onx(1), onx(-1), ony(1), ony(-1)])
+        for copy in first + spread[1]:
+            copy.start()
+    @pl.when(step == 5)
+    def _():
+        for k, copy in zip((1, -1), first):
+            copy.wait_recv()
+            for c in spread[1 - k]:
+                c.start()
+    @pl.loop(0, 30)
+    def _(c):
+        for r in range(9):
+            v = corr[:, pl.ds(pl.multiple_of((c * 9 + r) * 128, 128), 128)].astype(F32)
+            tmp[pl.ds(pl.multiple_of((c * 9 + r) * 16, 16), 16), :] = v
+    @pl.loop(0, G // 4)
+    def _(i):
+        for u in range(2):
+            for j in range(3):
+                for h in range(2):
+                    v = tmp[pl.ds(j * 16 + 4 * i + 2 * u + h, PR, stride=48), :].astype(BF)
+                    o_ref[2 * i + u, :, j * 256 + h * 128:j * 256 + h * 128 + 128] = v
+    @pl.when(step == pl.num_programs(0) - 1)
+    def _():
+        local.wait()
+        for group in spread:
+            for copy in group:
+                copy.wait_recv()
+        for copy in first + spread[0] + spread[1] + spread[2]:
+            copy.wait_send()
+
+
+def halo(own, corr, nx, ny):
     dma = pltpu.SemaphoreType.DMA
+    hbm = pl.BlockSpec(memory_space=pltpu.HBM)
     return pl.pallas_call(
         functools.partial(halo_body, nx, ny),
-        out_shape=jax.ShapeDtypeStruct((3, 3, A, 256), BF),
-        in_specs=[pl.BlockSpec(memory_space=pltpu.VMEM)],
-        out_specs=pl.BlockSpec(memory_space=pltpu.VMEM),
-        scratch_shapes=[dma((2,)), dma((2,)), dma((2, 3)), dma((2, 3))],
-        compiler_params=pltpu.CompilerParams(collective_id=0, has_side_effects=True),
+        grid=(A // G,),
+        out_shape=[jax.ShapeDtypeStruct((3, 3, A, 256), BF), jax.ShapeDtypeStruct((A // 2, PR, 768), BF)],
+        in_specs=[hbm, pl.BlockSpec((G, 34560), lambda s: (s, 0))],
+        out_specs=[hbm, pl.BlockSpec((G // 2, PR, 768), lambda s: (s, 0, 0))],
+        scratch_shapes=[pltpu.VMEM((288 * 16, 128), F32), dma, dma((2,)), dma((2,)), dma((2, 3)), dma((2, 3))],
+        compiler_params=pltpu.CompilerParams(collective_id=0, has_side_effects=True, vmem_limit_bytes=40 << 20),
         name="halo",
-    )(own)
+    )(own, corr)
 
 
 def exchange_body(nx, ny, part, pos, out, mine, near, edge, far, chosen, sent, mid, sm, s1, r1, s2, r2, s3, r3, s4, r4):
@@ -295,7 +309,7 @@
     return pl.pallas_call(
         functools.partial(exchange_body, nx, ny),
         out_shape=jax.ShapeDtypeStruct((nx, ny, 8, 128), BF),
-        in_specs=[pl.BlockSpec(memory_space=pl.ANY), vmem], out_specs=vmem,
+        in_specs=[pl.BlockSpec(memory_space=pltpu.HBM), vmem], out_specs=vmem,
         scratch_shapes=[pltpu.VMEM((3, A, 256), BF), pltpu.VMEM((2, 3, A, 256), BF), pltpu.VMEM((2, A, 256), BF), pltpu.VMEM((2, A, 256), BF),
                         pltpu.VMEM((nx * ny * 8, 2 * A), BF), pltpu.VMEM((nx, ny, 8, 128), BF),
                         pltpu.VMEM((nx, ny, 8, 128), BF),
@@ -308,11 +322,10 @@
 def on_device(density, neighbours, correlations, weight_first, bias_first, weight_second, bias_second,
               weight_third, bias_third, readout, destination):
     nx, ny = lax.axis_size("gx"), lax.axis_size("gy")
-    sel, mask = consts()
-    nbr = neighbours.reshape(A * NK)
-    ext = halo(density.reshape(A, 256), nx, ny).reshape(9 * A, 256)
+    nbr = neighbours.reshape(A, NK)
+    ext, o = halo(density.reshape(A, 256), relay(correlations), nx, ny)
     row = lambda v: v.reshape(1, H)
-    energy, slope, o = k1(nbr, ext, sel, relay(correlations), mask, weight_first, row(bias_first), weight_second,
+    energy, slope = k1(nbr, ext.reshape(9 * A, 256), consts(), o, weight_first, row(bias_first), weight_second,
                           row(bias_second), weight_third, row(bias_third), row(readout))
     part = k3(nbr, slope, o, fold_of(), 8).reshape(3, 3, A, 256)
     target = destination.reshape(A)

time: 141 us -> 148 us (1.050)
  Pallas kernels: 135 us -> 141 us
    pallas_call x1, Pallas kernels: 20.1 us -> 33.3 us  [halo(): pl.pallas_call(functools.partial(halo_body, nx, ny), grid=(A // G,), out_...]
    pallas_call x1, Pallas kernels: 54.4 us -> 44.6 us  [k1(): pl.pallas_call(functools.partial(k1_body, unroll), grid_spec=pltpu.Prefet...]
    unnamed x5 -> x11, local copies, waits for them, and re-layouts: 2.11 us -> 3.95 us
    pallas_call x1, Pallas kernels: 35.1 us -> 36.9 us  [k3(): pl.pallas_call(functools.partial(k3_body, unroll), grid_spec=pltpu.Prefet...]
where the time goes in v5:
time: 148 us; the launch traced here: 147 us
  Pallas kernels  141 us (95%)
  local copies, waits for them, and re-layouts  3.95 us (3%)
    pallas_call x1, Pallas kernels, k1(): pl.pallas_call(functools.partial(k1_body, unroll), grid_spec=pltpu.Prefet...  44.6 us
    pallas_call x1, Pallas kernels, k3(): pl.pallas_call(functools.partial(k3_body, unroll), grid_spec=pltpu.Prefet...  36.9 us
    pallas_call x1, Pallas kernels, halo(): pl.pallas_call(functools.partial(halo_body, nx, ny), grid=(A // G,), out_...  33.3 us
    pallas_call x1, Pallas kernels, exchange(): pl.pallas_call(functools.partial(exchange_body, nx, ny), out_shape=jax.Sh...  26.4 us
    unnamed x11, local copies, waits for them, and re-layouts  3.95 us

profile of v5, /device:TPU:1, one launch (start us, length us, event | category | flops | bytes accessed | tf_op | source)
XLA Modules:
  0.0 146.8 jit_solution(14333566256217447098)
XLA Ops:
  0.6 0.0 copy-start.2
  0.6 0.9 copy-done.2
  1.5 0.0 copy-start.3
  1.5 33.3 %halo.1 = (bf16[3,3,256,256]{3,2,1,0:T(8,128)(2,1)S(1)}, bf16[128,96,768]{2,1,0:T(8,128)(2,1)}) custom-call(bf16[256,256]{1,0:T(8,128)(2,1)S(1)} %bitcast.24, bf16[256,34560]{1,0:T(8,128)(2,1)} %bitcast.25), custom_call_target="tpu_custom_call" | custom-call | tf_op jit(solution)/shard_map/halo/pallas_call | solution.py:248
  34.9 0.0 copy-start.1
  34.9 1.0 copy-done.1
  35.9 0.0 copy-done.3
  35.9 0.8 copy.17
  36.7 44.6 %descriptor.1 = (f32[1,256]{1,0:T(1,128)}, f32[96,256,128]{2,1,0:T(8,128)}) custom-call(s32[256,24]{1,0:T(8,128)} %bitcast.26, bf16[2304,256]{1,0:T(8,128)(2,1)} %bitcast.23, bf16[256,2048]{1,0:T(8,128)(2,1)} %constant.8.clone.sel, bf16[128,96,768]{2,1,0:T(8,128)(2,1)} %get-tuple-element.7.o_ref, bf16[8100,256]{1,0:T(8,128)(2,1)} %w1_hbm.1, ...), custom_call_target="tpu_custom_call" | custom-call | tf_op jit(solution)/shard_map/descriptor/pallas_call | solution.py:100
  81.3 0.0 copy-start.4
  81.3 36.9 %hamilton.1 = bf16[2304,256]{1,0:T(8,128)(2,1)} custom-call(s32[256,24]{1,0:T(8,128)} %bitcast.27, f32[96,256,128]{2,1,0:T(8,128)} %get-tuple-element.9.s_ref, bf16[128,96,768]{2,1,0:T(8,128)(2,1)} %get-tuple-element.7.o_ref, bf16[2048,256]{1,0:T(8,128)(2,1)} %constant.9.clone.fold), custom_call_target="tpu_custom_call" | custom-call | tf_op jit(solution)/shard_map/hamilton/pallas_call | solution.py:163
  118.2 0.0 copy-done.4
  118.2 0.1 convert_reduce_fusion
  118.3 0.0 copy-start
  118.3 1.3 copy-done
  119.6 26.4 %exchange.1 = bf16[8,16,8,128]{3,2,1,0:T(8,128)(2,1)S(1)} custom-call(bf16[3,3,256,256]{3,2,1,0:T(8,128)(2,1)S(1)} %bitcast.22, s32[1,256]{1,0:T(1,128)S(1)} %bitcast_add_fusion.pos), custom_call_target="tpu_custom_call" | custom-call | tf_op jit(solution)/shard_map/exchange/pallas_call | solution.py:309
  146.0 0.8 convert.6
  (1 shorter events, 0.0 us)
Async XLA Ops:
  0.6 0.9 copy-start.2
  1.5 34.4 %copy-start.3 = (s32[1,1,256,24]{2,3,1,0:T(8,128)S(1)}, s32[1,1,256,24]{2,3,1,0:T(8,128)}, u32[]{:S(2)}) copy-start(s32[1,1,256,24]{2,3,1,0:T(8,128)} %param.14) | copy-start | bytes 73732
  34.9 1.0 copy-start.1
  81.3 36.9 %copy-start.4 = (s32[1,1,256,1]{2,3,1,0:T(1,128)S(1)}, s32[1,1,256,1]{2,3,1,0:T(1,128)}, u32[]{:S(2)}) copy-start(s32[1,1,256,1]{2,3,1,0:T(1,128)} %param.23) | copy-start | bytes 3076
  118.3 1.3 copy-start

commit v6 on v5

--- a/solution.py
+++ b/solution.py
@@ -20,7 +20,7 @@
     z = jnp.zeros_like(x)
     return jnp.concatenate([jnp.concatenate([x, z], 1), jnp.concatenate([z, y], 1)], 0)
 
-def k1_body(unroll, nbr, ext, sel, o_ref, w1_hbm, b1, w2, b2, w3, b3, ro, e_ref, s_hbm,
+def k1_body(unroll, nbr, ext, sel, o0, o1, o2, w1_hbm, b1, w2, b2, w3, b3, ro, e_ref, s_hbm,
             table, tmp, mask, d_ref, w1, wide, rows, w_sem, s_sem):
     step = pl.program_id(0)
     fetch = pltpu.make_async_copy(w1_hbm, w1, w_sem)
@@ -43,11 +43,11 @@
     def bdiag(i, h, j):
         return jnp.concatenate([table[nbr[step * G + 2 * i + h, 8 * j + kk]] * mask[kk] for kk in range(8)], 0)
     def pair(i):
-        o = [[o_ref[i, :, j * 256 + h * 128:j * 256 + h * 128 + 128] for j in range(3)] for h in range(2)]
+        o = [[v[i, :, h * 128:h * 128 + 128] for v in (o0, o1, o2)] for h in range(2)]
         ot = [[jnp.concatenate([o[h][j], pad], 0).T for j in range(3)] for h in range(2)]
         p = []
         for j in range(3):
-            p.append(dot(o_ref[i, :, j * 256:(j + 1) * 256], diag(bdiag(i, 0, j), bdiag(i, 1, j))).astype(BF))
+            p.append(dot((o0, o1, o2)[j][i], diag(bdiag(i, 0, j), bdiag(i, 1, j))).astype(BF))
         d = dot(jnp.concatenate(p, 1), jnp.concatenate([diag(ot[0][j], ot[1][j]) for j in range(3)], 0))
         for h in range(2):
             d2[pl.ds(step * G + 2 * i + h, PR, stride=A), :] = d[:, h * 128:(h + 1) * 128]
@@ -103,7 +103,7 @@
             num_scalar_prefetch=1, grid=(A // G,),
             in_specs=[pl.BlockSpec((9 * A, 256), lambda s, n: (0, 0)),
                       pl.BlockSpec((256, 2048), lambda s, n: (0, 0)),
-                      pl.BlockSpec((G // 2, PR, 768), lambda s, n: (s, 0, 0)),
+                      *[pl.BlockSpec((G // 2, PR, 256), lambda s, n: (s, 0, 0))] * 3,
                       pl.BlockSpec(memory_space=pl.ANY),
                       row(), mat(), row(), mat(), row(), row()],
             out_specs=[pl.BlockSpec((1, A), lambda s, n: (0, 0)),
@@ -115,7 +115,7 @@
         out_shape=[jax.ShapeDtypeStruct((1, A), F32), jax.ShapeDtypeStruct((PR, A, 128), F32)],
         compiler_params=pltpu.CompilerParams(vmem_limit_bytes=60 << 20, dimension_semantics=("arbitrary",)),
         name="descriptor",
-    )(nbr, ext, sel, o, w1, b1, w2, b2, w3, b3, ro)
+    )(nbr, ext, sel, *o, w1, b1, w2, b2, w3, b3, ro)
 
 def consts():
     i = np.arange(256)[:, None]; c = np.arange(2048)[None]
@@ -125,19 +125,19 @@
 def relay(corr):
     return corr.reshape(256, 34560)
 
-def k3_body(unroll, nbr, s_ref, o_ref, fold, out_ref, acc):
+def k3_body(unroll, nbr, s0, s1, s2, o0, o1, o2, fold, out_ref, acc):
     step = pl.program_id(0)
     @pl.when(step == 0)
     def _():
         @pl.loop(0, 144)
         def _(c):
             acc[pl.ds(c * 16, 16)] = jnp.zeros((16, 16, 128), F32)
-    s2 = s_ref.reshape(PR * G, 128)
+    slopes = [v.reshape(PR // 3 * G, 128) for v in (s0, s1, s2)]
     pad = jnp.zeros((128 - PR, 128), BF)
     lane = lax.broadcasted_iota(jnp.int32, (16, 128), 1) // 16
     def pair(i):
-        st = [jnp.concatenate([s2[pl.ds(2 * i + h, PR, stride=G), :].astype(BF), pad], 0).T for h in range(2)]
-        o = [[jnp.concatenate([o_ref[i, :, j * 256 + h * 128:j * 256 + h * 128 + 128], pad], 0) for j in range(3)] for h in range(2)]
+        st = [jnp.concatenate([v[pl.ds(2 * i + h, PR // 3, stride=G), :].astype(BF) for v in slopes] + [pad], 0).T for h in range(2)]
+        o = [[jnp.concatenate([v[i, :, h * 128:h * 128 + 128], pad], 0) for v in (o0, o1, o2)] for h in range(2)]
         ot = jnp.concatenate([jnp.concatenate([o[0][j].T, o[1][j].T], 1) for j in range(3)], 0)
         lt = dot(ot, diag(*st)).astype(BF)
         for j in range(3):
@@ -164,15 +164,15 @@
         functools.partial(k3_body, unroll),
         grid_spec=pltpu.PrefetchScalarGridSpec(
             num_scalar_prefetch=1, grid=(A // G,),
-            in_specs=[pl.BlockSpec((PR, G, 128), lambda s, n: (0, s, 0)),
-                      pl.BlockSpec((G // 2, PR, 768), lambda s, n: (s, 0, 0)),
+            in_specs=[*[pl.BlockSpec((PR // 3, G, 128), functools.partial(lambda c, s, n: (c, s, 0), c)) for c in range(3)],
+                      *[pl.BlockSpec((G // 2, PR, 256), lambda s, n: (s, 0, 0))] * 3,
                       pl.BlockSpec((2048, 256), lambda s, n: (0, 0))],
             out_specs=pl.BlockSpec((9 * A, 256), lambda s, n: (0, 0)),
             scratch_shapes=[pltpu.VMEM((9 * A, 16, 128), F32)]),
         out_shape=jax.ShapeDtypeStruct((9 * A, 256), BF),
         compiler_params=pltpu.CompilerParams(vmem_limit_bytes=60 << 20),
         name="hamilton",
-    )(nbr, s, ot, fold)
+    )(nbr, s, s, s, *ot, fold)
 
 def fold_of():
     i = np.arange(2048)[:, None]; c = np.arange(256)[None]
@@ -196,7 +196,7 @@
     return copy
 
 
-def halo_body(nx, ny, own, corr, out, o_ref, tmp, keep, sy, ry, sx, rx):
+def halo_body(nx, ny, own, c0, c1, c2, out, o0, o1, o2, tmp, keep, sy, ry, sx, rx):
     step = pl.program_id(0)
     x, y = lax.axis_index("gx"), lax.axis_index("gy")
     onx = lambda k: {"gx": lax.rem(x + k + nx, nx)}
@@ -220,18 +220,19 @@
             copy.wait_recv()
             for c in spread[1 - k]:
                 c.start()
-    @pl.loop(0, 30)
-    def _(c):
-        for r in range(9):
-            v = corr[:, pl.ds(pl.multiple_of((c * 9 + r) * 128, 128), 128)].astype(F32)
-            tmp[pl.ds(pl.multiple_of((c * 9 + r) * 16, 16), 16), :] = v
+    for part, corr in enumerate((c0, c1, c2)):
+        @pl.loop(0, 10)
+        def _(c):
+            for r in range(9):
+                v = corr[:, pl.ds(pl.multiple_of((c * 9 + r) * 128, 128), 128)].astype(F32)
+                tmp[pl.ds(pl.multiple_of((part * 90 + c * 9 + r) * 16, 16), 16), :] = v
     @pl.loop(0, G // 4)
     def _(i):
         for u in range(2):
             for j in range(3):
                 for h in range(2):
                     v = tmp[pl.ds(j * 16 + 4 * i + 2 * u + h, PR, stride=48), :].astype(BF)
-                    o_ref[2 * i + u, :, j * 256 + h * 128:j * 256 + h * 128 + 128] = v
+                    (o0, o1, o2)[j][2 * i + u, :, h * 128:h * 128 + 128] = v
     @pl.when(step == pl.num_programs(0) - 1)
     def _():
         local.wait()
@@ -248,13 +249,13 @@
     return pl.pallas_call(
         functools.partial(halo_body, nx, ny),
         grid=(A // G,),
-        out_shape=[jax.ShapeDtypeStruct((3, 3, A, 256), BF), jax.ShapeDtypeStruct((A // 2, PR, 768), BF)],
-        in_specs=[hbm, pl.BlockSpec((G, 34560), lambda s: (s, 0))],
-        out_specs=[hbm, pl.BlockSpec((G // 2, PR, 768), lambda s: (s, 0, 0))],
+        out_shape=[jax.ShapeDtypeStruct((3, 3, A, 256), BF), *[jax.ShapeDtypeStruct((A // 2, PR, 256), BF)] * 3],
+        in_specs=[hbm, *[pl.BlockSpec((G, 11520), functools.partial(lambda c, s: (s, c), c)) for c in range(3)]],
+        out_specs=[hbm, *[pl.BlockSpec((G // 2, PR, 256), lambda s: (s, 0, 0))] * 3],
         scratch_shapes=[pltpu.VMEM((288 * 16, 128), F32), dma, dma((2,)), dma((2,)), dma((2, 3)), dma((2, 3))],
         compiler_params=pltpu.CompilerParams(collective_id=0, has_side_effects=True, vmem_limit_bytes=40 << 20),
         name="halo",
-    )(own, corr)
+    )(own, corr, corr, corr)
 
 
 def exchange_body(nx, ny, part, pos, out, mine, near, edge, far, chosen, sent, mid, sm, s1, r1, s2, r2, s3, r3, s4, r4):
@@ -323,7 +324,7 @@
               weight_third, bias_third, readout, destination):
     nx, ny = lax.axis_size("gx"), lax.axis_size("gy")
     nbr = neighbours.reshape(A, NK)
-    ext, o = halo(density.reshape(A, 256), relay(correlations), nx, ny)
+    ext, *o = halo(density.reshape(A, 256), relay(correlations), nx, ny)
     row = lambda v: v.reshape(1, H)
     energy, slope = k1(nbr, ext.reshape(9 * A, 256), consts(), o, weight_first, row(bias_first), weight_second,
                           row(bias_second), weight_third, row(bias_third), row(readout))

time: 148 us -> 150 us (1.014)
  local copies, waits for them, and re-layouts: 3.95 us -> 9.23 us
  Pallas kernels: 141 us -> 138 us
    unnamed x11 -> x15, local copies, waits for them, and re-layouts: 3.95 us -> 9.23 us
    pallas_call x1, Pallas kernels: 33.3 us -> 30.9 us  [halo(): pl.pallas_call(functools.partial(halo_body, nx, ny), grid=(A // G,), out_...]
where the time goes in v6:
time: 150 us; the launch traced here: 149 us
  Pallas kernels  138 us (92%)
  local copies, waits for them, and re-layouts  9.23 us (6%)
    pallas_call x1, Pallas kernels, k1(): pl.pallas_call(functools.partial(k1_body, unroll), grid_spec=pltpu.Prefet...  44.8 us
    pallas_call x1, Pallas kernels, k3(): pl.pallas_call(functools.partial(k3_body, unroll), grid_spec=pltpu.Prefet...  36.5 us
    pallas_call x1, Pallas kernels, halo(): pl.pallas_call(functools.partial(halo_body, nx, ny), grid=(A // G,), out_...  30.9 us
    pallas_call x1, Pallas kernels, exchange(): pl.pallas_call(functools.partial(exchange_body, nx, ny), out_shape=jax.Sh...  25.8 us
    unnamed x15, local copies, waits for them, and re-layouts  9.23 us

profile of v6, /device:TPU:1, one launch (start us, length us, event | category | flops | bytes accessed | tf_op | source)
XLA Modules:
  0.0 148.9 jit_solution(7387588563916319530)
XLA Ops:
  0.6 0.0 copy-start.4
  0.6 0.9 copy-done.4
  1.5 0.0 copy-start.5
  1.5 30.9 %halo.1 = (bf16[3,3,256,256]{3,2,1,0:T(8,128)(2,1)S(1)}, bf16[128,96,256]{2,1,0:T(8,128)(2,1)S(1)}, bf16[128,96,256]{2,1,0:T(8,128)(2,1)S(1)}, bf16[128,96,256]{2,1,0:T(8,128)(2,1)}) custom-call(bf16[256,256]{1,0:T(8,128)(2,1)S(1)} %bitcast.24, bf16[256,34560]{1,0:T(8,128)(2,1)} %bitcast.25, bf16[256,34560]{1,0:T(8,128)(2,1)} %bitcast.26, ...), custom_call_target="tpu_custom_call" | custom-call | tf_op jit(solution)/shard_map/halo/pallas_call | solution.py:249
  32.5 0.0 copy-start
  32.5 2.6 %copy-done = bf16[128,96,256]{2,1,0:T(8,128)(2,1)} copy-done((bf16[128,96,256]{2,1,0:T(8,128)(2,1)}, bf16[128,96,256]{2,1,0:T(8,128)(2,1)S(1)}, u32[]{:S(2)}) %copy-start) | copy-done | bytes 6291480
  35.1 0.0 copy-start.1
  35.1 2.7 %copy-done.1 = bf16[128,96,256]{2,1,0:T(8,128)(2,1)} copy-done((bf16[128,96,256]{2,1,0:T(8,128)(2,1)}, bf16[128,96,256]{2,1,0:T(8,128)(2,1)S(1)}, u32[]{:S(2)}) %copy-start.1) | copy-done | bytes 6291480
  37.8 0.0 copy-start.3
  37.8 1.0 copy-done.3
  38.8 0.0 copy-done.5
  38.8 0.8 copy.17
  39.6 44.8 %descriptor.1 = (f32[1,256]{1,0:T(1,128)}, f32[96,256,128]{2,1,0:T(8,128)}) custom-call(s32[256,24]{1,0:T(8,128)} %bitcast.28, bf16[2304,256]{1,0:T(8,128)(2,1)} %bitcast.23, bf16[256,2048]{1,0:T(8,128)(2,1)} %constant.8.clone.sel, bf16[128,96,256]{2,1,0:T(8,128)(2,1)} %copy-done, bf16[128,96,256]{2,1,0:T(8,128)(2,1)} %copy-done.1, ...), custom_call_target="tpu_custom_call" | custom-call | tf_op jit(solution)/shard_map/descriptor/pallas_call | solution.py:100
  84.3 0.0 copy-start.6
  84.3 36.5 %hamilton.1 = bf16[2304,256]{1,0:T(8,128)(2,1)} custom-call(s32[256,24]{1,0:T(8,128)} %bitcast.29, f32[96,256,128]{2,1,0:T(8,128)} %get-tuple-element.13.s0.s1.s2, f32[96,256,128]{2,1,0:T(8,128)} %get-tuple-element.13.s0.s1.s2, f32[96,256,128]{2,1,0:T(8,128)} %get-tuple-element.13.s0.s1.s2, bf16[128,96,256]{2,1,0:T(8,128)(2,1)} %copy-done, ...), custom_call_target="tpu_custom_call" | custom-call | tf_op jit(solution)/shard_map/hamilton/pallas_call | solution.py:163
  120.9 0.0 copy-done.6
  120.9 0.1 convert_reduce_fusion
  121.0 0.0 copy-start.2
  121.0 1.3 copy-done.2
  122.3 25.8 %exchange.1 = bf16[8,16,8,128]{3,2,1,0:T(8,128)(2,1)S(1)} custom-call(bf16[3,3,256,256]{3,2,1,0:T(8,128)(2,1)S(1)} %bitcast.22, s32[1,256]{1,0:T(1,128)S(1)} %bitcast_add_fusion.pos), custom_call_target="tpu_custom_call" | custom-call | tf_op jit(solution)/shard_map/exchange/pallas_call | solution.py:310
  148.1 0.8 convert.6
  (1 shorter events, 0.0 us)
Async XLA Ops:
  0.6 0.9 copy-start.4
  1.5 37.3 %copy-start.5 = (s32[1,1,256,24]{2,3,1,0:T(8,128)S(1)}, s32[1,1,256,24]{2,3,1,0:T(8,128)}, u32[]{:S(2)}) copy-start(s32[1,1,256,24]{2,3,1,0:T(8,128)} %param.14) | copy-start | bytes 73732
  32.5 2.6 %copy-start = (bf16[128,96,256]{2,1,0:T(8,128)(2,1)}, bf16[128,96,256]{2,1,0:T(8,128)(2,1)S(1)}, u32[]{:S(2)}) copy-start(bf16[128,96,256]{2,1,0:T(8,128)(2,1)S(1)} %get-tuple-element.9.o0) | copy-start | bytes 18874372
  35.1 2.7 %copy-start.1 = (bf16[128,96,256]{2,1,0:T(8,128)(2,1)}, bf16[128,96,256]{2,1,0:T(8,128)(2,1)S(1)}, u32[]{:S(2)}) copy-start(bf16[128,96,256]{2,1,0:T(8,128)(2,1)S(1)} %get-tuple-element.10.o1) | copy-start | bytes 18874372
  37.8 1.0 copy-start.3
  84.3 36.5 %copy-start.6 = (s32[1,1,256,1]{2,3,1,0:T(1,128)S(1)}, s32[1,1,256,1]{2,3,1,0:T(1,128)}, u32[]{:S(2)}) copy-start(s32[1,1,256,1]{2,3,1,0:T(1,128)} %param.23) | copy-start | bytes 3076
  121.0 1.3 copy-start.2

commit v7 on v4

--- a/solution.py
+++ b/solution.py
@@ -20,14 +20,17 @@
     z = jnp.zeros_like(x)
     return jnp.concatenate([jnp.concatenate([x, z], 1), jnp.concatenate([z, y], 1)], 0)
 
-def k1_body(unroll, nbr, ext, sel, corr, mask, w1_hbm, b1, w2, b2, w3, b3, ro, e_ref, s_hbm, o_ref,
-            table, tmp, d_ref, w1, wide, rows, w_sem, s_sem):
+def k1_body(unroll, nbr, ext, sel, corr, w1_hbm, b1, w2, b2, w3, b3, ro, e_ref, s_hbm, o_ref,
+            table, tmp, mask, d_ref, w1, wide, rows, w_sem, s_sem):
     step = pl.program_id(0)
     fetch = pltpu.make_async_copy(w1_hbm, w1, w_sem)
     @pl.when(step == 0)
     def _():
         fetch.start()
         tmp[pl.ds(270 * 16, 18 * 16), :] = jnp.zeros((18 * 16, 128), F32)
+        lane = lax.broadcasted_iota(jnp.int32, (16, 128), 1) >> 4
+        for kk in range(8):
+            mask[kk] = jnp.where(lane == kk, 1.0, 0.0).astype(BF)
         @pl.loop(0, 9)
         def _(b):
             own = ext[pl.ds(pl.multiple_of(b * 256, 256), 256), :]
@@ -100,7 +103,7 @@
             copy.wait()
 
 PC = 16
-def k1(nbr, ext, sel, corr, mask, w1, b1, w2, b2, w3, b3, ro, unroll=8):
+def k1(nbr, ext, sel, corr, w1, b1, w2, b2, w3, b3, ro, unroll=8):
     row = lambda: pl.BlockSpec((1, H), lambda s, n: (0, 0))
     mat = lambda: pl.BlockSpec((H, H), lambda s, n: (0, 0))
     return pl.pallas_call(
@@ -110,13 +113,13 @@
             in_specs=[pl.BlockSpec((9 * A, 256), lambda s, n: (0, 0)),
                       pl.BlockSpec((256, 2048), lambda s, n: (0, 0)),
                       pl.BlockSpec((G, 34560), lambda s, n: (s, 0)),
-                      pl.BlockSpec((8, 16, 128), lambda s, n: (0, 0, 0)),
                       pl.BlockSpec(memory_space=pl.ANY),
                       row(), mat(), row(), mat(), row(), row()],
             out_specs=[pl.BlockSpec((1, A), lambda s, n: (0, 0)),
                        pl.BlockSpec(memory_space=pl.ANY),
                        pl.BlockSpec((G // 2, PR, 768), lambda s, n: (s, 0, 0))],
             scratch_shapes=[pltpu.VMEM((9 * A, 16, 128), BF), pltpu.VMEM((288 * 16, 128), F32),
+                            pltpu.VMEM((8, 16, 128), BF),
                             pltpu.VMEM((PR, A, 128), F32), pltpu.VMEM((NP * NP, H), BF),
                             pltpu.VMEM((NP // 2, 256, H), BF), pltpu.VMEM((PC * NP + 8, H), F32),
                             pltpu.SemaphoreType.DMA, pltpu.SemaphoreType.DMA((PR // PC,))]),
@@ -124,14 +127,12 @@
                    jax.ShapeDtypeStruct((A // 2, PR, 768), BF)],
         compiler_params=pltpu.CompilerParams(vmem_limit_bytes=60 << 20, dimension_semantics=("arbitrary",)),
         name="descriptor",
-    )(nbr, ext, sel, corr, mask, w1, b1, w2, b2, w3, b3, ro)
+    )(nbr, ext, sel, corr, w1, b1, w2, b2, w3, b3, ro)
 
 def consts():
     i = np.arange(256)[:, None]; c = np.arange(2048)[None]
     sel = (((i >> 4) == (c >> 7)) & ((i & 15) == (c & 15))).astype(BF)
-    k = jnp.arange(8)[:, None, None]; l = jnp.arange(128)[None, None]
-    mask = jnp.broadcast_to(((l >> 4) == k), (8, 16, 128)).astype(BF)
-    return jnp.asarray(sel), jnp.asarray(mask)
+    return jnp.asarray(sel)
 
 def relay(corr):
     return corr.reshape(256, 34560)
@@ -300,7 +301,7 @@
                         pltpu.VMEM((nx * ny * 8, 2 * A), BF), pltpu.VMEM((nx, ny, 8, 128), BF),
                         pltpu.VMEM((nx, ny, 8, 128), BF),
                         dma, dma((2, 3)), dma((2, 3)), dma((2,)), dma((2,)), dma((nx,)), dma((nx,)), dma((ny,)), dma((ny,))],
-        compiler_params=pltpu.CompilerParams(collective_id=1, has_side_effects=True, vmem_limit_bytes=40 << 20),
+        compiler_params=pltpu.CompilerParams(collective_id=1, has_side_effects=True, vmem_limit_bytes=63 << 20),
         name="exchange",
     )(part, position)
 
@@ -308,11 +309,11 @@
 def on_device(density, neighbours, correlations, weight_first, bias_first, weight_second, bias_second,
               weight_third, bias_third, readout, destination):
     nx, ny = lax.axis_size("gx"), lax.axis_size("gy")
-    sel, mask = consts()
+    sel = consts()
     nbr = neighbours.reshape(A * NK)
     ext = halo(density.reshape(A, 256), nx, ny).reshape(9 * A, 256)
     row = lambda v: v.reshape(1, H)
-    energy, slope, o = k1(nbr, ext, sel, relay(correlations), mask, weight_first, row(bias_first), weight_second,
+    energy, slope, o = k1(nbr, ext, sel, relay(correlations), weight_first, row(bias_first), weight_second,
                           row(bias_second), weight_third, row(bias_third), row(readout))
     part = k3(nbr, slope, o, fold_of(), 8).reshape(3, 3, A, 256)
     target = destination.reshape(A)

time: 141 us -> 142 us (level)
  local copies, waits for them, and re-layouts: 3.45 us -> 1.56 us
  other arithmetic: 0.96 us -> 2.47 us
where the time goes in v7:
time: 142 us; the launch traced here: 141 us
  Pallas kernels  136 us (96%)
  other arithmetic  2.47 us (2%)
  local copies, waits for them, and re-layouts  1.56 us (1%)
    pallas_call x1, Pallas kernels, k1(): pl.pallas_call(functools.partial(k1_body, unroll), grid_spec=pltpu.Prefet...  54.4 us
    pallas_call x1, Pallas kernels, k3(): pl.pallas_call(functools.partial(k3_body, unroll), grid_spec=pltpu.Prefet...  35.1 us
    pallas_call x1, Pallas kernels, exchange(): pl.pallas_call(functools.partial(exchange_body, nx, ny), out_shape=jax.Sh...  26.6 us
    pallas_call x1, Pallas kernels, halo(): pl.pallas_call(functools.partial(halo_body, nx, ny), out_shape=jax.ShapeD...  20.1 us

profile of v7, /device:TPU:1, one launch (start us, length us, event | category | flops | bytes accessed | tf_op | source)
XLA Modules:
  0.0 140.9 jit_solution(10072012419610653041)
XLA Ops:
  0.6 0.8 copy.18
  1.5 0.7 reshape.75.nbr
  2.2 20.1 %halo.1 = bf16[3,3,256,256]{3,2,1,0:T(8,128)(2,1)} custom-call(bf16[256,256]{1,0:T(8,128)(2,1)} %bitcast.27), custom_call_target="tpu_custom_call" | custom-call | tf_op jit(solution)/shard_map/halo/pallas_call | solution.py:236
  22.3 54.4 %descriptor.1 = (f32[1,256]{1,0:T(1,128)}, f32[96,256,128]{2,1,0:T(8,128)}, bf16[128,96,768]{2,1,0:T(8,128)(2,1)}) custom-call(s32[6144]{0:T(1024)} %reshape.75.nbr, bf16[2304,256]{1,0:T(8,128)(2,1)} %bitcast.25, bf16[256,2048]{1,0:T(8,128)(2,1)} %constant.8.clone.sel, bf16[256,34560]{1,0:T(8,128)(2,1)} %bitcast.23, bf16[8100,256]{1,0:T(8,128)(2,1)} %w1_hbm.1, ...), custom_call_target="tpu_custom_call" | custom-call | tf_op jit(solution)/shard_map/descriptor/pallas_call | solution.py:109
  76.7 0.0 copy-start
  76.7 35.1 %hamilton.1 = bf16[2304,256]{1,0:T(8,128)(2,1)} custom-call(s32[6144]{0:T(1024)} %reshape.75.nbr, f32[96,256,128]{2,1,0:T(8,128)} %get-tuple-element.6.s_ref, bf16[128,96,768]{2,1,0:T(8,128)(2,1)} %get-tuple-element.7.o_ref, bf16[2048,256]{1,0:T(8,128)(2,1)} %constant.9.clone.fold), custom_call_target="tpu_custom_call" | custom-call | tf_op jit(solution)/shard_map/hamilton/pallas_call | solution.py:176
  111.8 0.0 copy-done
  111.8 0.1 convert_reduce_fusion
  111.9 0.6 bitcast_add_fusion.pos
  112.5 26.6 %exchange.1 = bf16[8,16,8,128]{3,2,1,0:T(8,128)(2,1)} custom-call(bf16[3,3,256,256]{3,2,1,0:T(8,128)(2,1)} %bitcast.24, s32[1,256]{1,0:T(1,128)} %bitcast_add_fusion.pos), custom_call_target="tpu_custom_call" | custom-call | tf_op jit(solution)/shard_map/exchange/pallas_call | solution.py:296
  139.1 1.8 %convert.6 = f32[8,16,8,128]{3,2,1,0:T(8,128)} convert(bf16[8,16,8,128]{3,2,1,0:T(8,128)(2,1)} %exchange.1) | non-fusion elementwise | flops 131072 | bytes 786432
Async XLA Ops:
  76.7 35.2 %copy-start = (s32[1,1,256,1]{2,3,1,0:T(1,128)S(1)}, s32[1,1,256,1]{2,3,1,0:T(1,128)}, u32[]{:S(2)}) copy-start(s32[1,1,256,1]{2,3,1,0:T(1,128)} %param.23) | copy-start | bytes 3076
